TPU v7x, 256 devices: a whole 4x4x8 slice. The times are simulated.
256 devices in a mesh: gx: 16 (over y, x), gy: 16 (over z, core).
Axes of the slice: x: 4, y: 4, z: 8, core: 2. Of those that a mesh axis runs over, the one named last changes fastest.
Arguments:
- source: float32 [128, 512, 256], P('gx', 'gy'), may hold values from -4 to 4
- damping: float32 [128, 512, 256], P('gx', 'gy'), may hold values from 0.0005 to 0.02
- coarse_one: float32 [27, 64, 256, 128], P(None, 'gx', 'gy'), may hold values from -1.5 to 22
- coarse_two: float32 [27, 32, 128, 64], P(None, 'gx', 'gy'), may hold values from -3 to 44
- coarse_three: float32 [27, 16, 64, 32], P(None, 'gx', 'gy'), may hold values from -6 to 87
Outputs:
- preconditioned: float32 [128, 512, 256], P('gx', 'gy')
All inputs are finite; a program needn't handle non-finite values.
Results may differ from a plain program's by a relative error of at most 0.00008.
Values sent between devices are 32-bit elements; how exact they have to be, the bound alone decides.
No kernel may reach another device: no remote copies, remote signals or barrier semaphores. Data moves between devices by JAX's collectives and lax.ppermute only.
A program may use at most 64 MiB of HBM per device.

v0:
```python
import jax
import jax.numpy as jnp
from jax import lax
from jax.sharding import PartitionSpec as P

NU = 4
CSWEEPS = 8


RELAXATION = 0.8
OFFSETS = tuple(
    (
        (shift_x, shift_y, shift_z)
        for shift_x in (-1, 0, 1)
        for shift_y in (-1, 0, 1)
        for shift_z in (-1, 0, 1)
    )
)


def extended_2(shard, sides, width):
    for axis, dim in sides:
        size, length = (lax.axis_size(axis), shard.shape[dim])
        up = [(i, (i + 1) % size) for i in range(size - 1)]
        down = [(j, i) for i, j in up]
        last = lax.slice_in_dim(shard, length - width, length, axis=dim)
        leading = lax.slice_in_dim(shard, 0, width, axis=dim)
        before = lax.ppermute(last, axis, up)
        after = lax.ppermute(leading, axis, down)
        shard = jnp.concatenate([before, shard, after], axis=dim)
    return shard


def pad_along(field, along_dim):
    widths = [(0, 0)] * field.ndim
    widths[along_dim] = (1, 1)
    return jnp.pad(field, widths)


def seven_point(extended, damping):
    extent_x, extent_y = (damping.shape[0], damping.shape[1])
    padded = pad_along(extended, 2)
    centre = extended[1 : extent_x + 1, 1 : extent_y + 1, :]
    beside = (
        extended[2 : extent_x + 2, 1 : extent_y + 1, :] + extended[0:extent_x, 1 : extent_y + 1, :]
    )
    beside = (
        beside
        + extended[1 : extent_x + 1, 2 : extent_y + 2, :]
        + extended[1 : extent_x + 1, 0:extent_y, :]
    )
    beside = (
        beside
        + padded[1 : extent_x + 1, 1 : extent_y + 1, 2:]
        + padded[1 : extent_x + 1, 1 : extent_y + 1, :-2]
    )
    return (6.0 + damping) * centre - beside


def twenty_seven(extended, coefficients):
    extent_x, extent_y, extent_z = (
        coefficients.shape[1],
        coefficients.shape[2],
        coefficients.shape[3],
    )
    padded = pad_along(extended, 2)
    summed = jnp.zeros(coefficients.shape[1:], jnp.float32)
    for number, (shift_x, shift_y, shift_z) in enumerate(OFFSETS):
        window = padded[
            1 + shift_x : 1 + shift_x + extent_x,
            1 + shift_y : 1 + shift_y + extent_y,
            1 + shift_z : 1 + shift_z + extent_z,
        ]
        summed = summed + coefficients[number] * window
    return summed


def restrict_along(extended, along_dim):
    coarse_count = (extended.shape[along_dim] - 2) // 2
    lower_far = lax.slice_in_dim(extended, 0, 2 * coarse_count, 2, along_dim)
    lower_near = lax.slice_in_dim(extended, 1, 2 * coarse_count + 1, 2, along_dim)
    upper_near = lax.slice_in_dim(extended, 2, 2 * coarse_count + 2, 2, along_dim)
    upper_far = lax.slice_in_dim(extended, 3, 2 * coarse_count + 2, 2, along_dim)
    return 0.25 * (lower_far + upper_far) + 0.75 * (lower_near + upper_near)


def prolong_along(extended, along_dim):
    coarse_count = extended.shape[along_dim] - 2
    centre = lax.slice_in_dim(extended, 1, coarse_count + 1, 1, along_dim)
    lower_side = lax.slice_in_dim(extended, 0, coarse_count, 1, along_dim)
    upper_side = lax.slice_in_dim(extended, 2, coarse_count + 2, 1, along_dim)
    even_cells = 0.75 * centre + 0.25 * lower_side
    odd_cells = 0.75 * centre + 0.25 * upper_side
    stacked = jnp.stack([even_cells, odd_cells], axis=along_dim + 1)
    target_shape = list(centre.shape)
    target_shape[along_dim] = 2 * coarse_count
    return stacked.reshape(target_shape)


def restrict_cells(extended):
    reduced = restrict_along(extended, 0)
    reduced = restrict_along(reduced, 1)
    return restrict_along(pad_along(reduced, 2), 2)


def prolong_cells(extended):
    grown = prolong_along(extended, 0)
    grown = prolong_along(grown, 1)
    return prolong_along(pad_along(grown, 2), 2)


def rims(field):
    return extended_2(field, (("gx", 0), ("gy", 1)), 1)


def faces(field):
    return extended_2(field, (("gx", 0), ("gy", 1)), 1)


def coarse_sweeps(source, coefficients, iterate, count):
    diagonal = coefficients[13]
    for repeat in range(count):
        iterate = (
            iterate + RELAXATION * (source - twenty_seven(rims(iterate), coefficients)) / diagonal
        )
    return iterate


def coarsest_level(source, coefficients):
    iterate = RELAXATION * source / coefficients[13]
    return coarse_sweeps(source, coefficients, iterate, CSWEEPS - 1)


def coarse_cycle(source, operators):
    coefficients = operators[0]
    if len(operators) == 1:
        return coarsest_level(source, coefficients)
    iterate = RELAXATION * source / coefficients[13]
    iterate = coarse_sweeps(source, coefficients, iterate, NU - 1)
    residual = source - twenty_seven(rims(iterate), coefficients)
    correction = coarse_cycle(restrict_cells(rims(residual)), operators[1:])
    iterate = iterate + prolong_cells(rims(correction))
    return coarse_sweeps(source, coefficients, iterate, NU)


def fine_sweeps(source, damping, iterate, count):
    for repeat in range(count):
        iterate = iterate + RELAXATION * (source - seven_point(faces(iterate), damping)) / (
            6.0 + damping
        )
    return iterate


def on_device(source, damping, coarse_one, coarse_two, coarse_three):
    iterate = RELAXATION * source / (6.0 + damping)
    iterate = fine_sweeps(source, damping, iterate, NU - 1)
    residual = source - seven_point(faces(iterate), damping)
    coarse_source = restrict_cells(rims(residual))
    correction = coarse_cycle(coarse_source, (coarse_one, coarse_two, coarse_three))
    iterate = iterate + prolong_cells(rims(correction))
    return fine_sweeps(source, damping, iterate, NU)


def solution(mesh):
    in_specs = (
        P("gx", "gy", None),
        P("gx", "gy", None),
        P(None, "gx", "gy", None),
        P(None, "gx", "gy", None),
        P(None, "gx", "gy", None),
    )
    out_specs = P("gx", "gy", None)
    return jax.shard_map(
        on_device, mesh=mesh, in_specs=in_specs, out_specs=out_specs, check_vma=False
    )
```

profile of v0, /device:TPU:103, one launch (start us, length us, event | category | flops | bytes accessed | tf_op | source)
XLA Modules:
  0.0 686.1 jit_solution(5587121824266323965)
XLA Ops:
  6.4 4.6 collective-permute-done
  11.0 6.7 collective-permute-start.3
  19.9 4.3 collective-permute-done.2
  38.5 4.3 collective-permute-done.6
  57.0 4.3 collective-permute-done.10
  75.6 4.3 collective-permute-done.14
  94.2 4.3 collective-permute-done.19
  116.9 4.2 collective-permute-done.23
  134.9 4.2 collective-permute-done.27
  152.9 4.2 collective-permute-done.31
  170.9 4.2 collective-permute-done.35
  189.1 4.2 collective-permute-done.39
  207.7 4.2 collective-permute-done.43
  286.0 5.5 collective-permute-start.60
  303.5 6.0 collective-permute-start.64
  321.4 6.0 collective-permute-start.68
  339.2 6.0 collective-permute-start.72
  357.0 6.0 collective-permute-start.76
  374.7 6.0 collective-permute-start.80
  392.5 6.0 collective-permute-start.84
  410.3 6.0 collective-permute-start.88
  426.3 6.0 collective-permute-start.92
  434.2 4.5 collective-permute-done.93
  533.6 4.2 collective-permute-done.115
  551.6 4.2 collective-permute-done.119
  569.6 4.2 collective-permute-done.123
  587.6 4.2 collective-permute-done.127
  605.6 4.2 collective-permute-done.131
  624.8 4.3 collective-permute-done.134
  643.4 4.3 collective-permute-done.138
  662.0 4.3 collective-permute-done.142
  680.6 4.3 collective-permute-done.146
  (485 shorter events, 529.5 us)
Async XLA Ops:
  4.2 6.8 collective-permute-start
  11.0 8.8 %collective-permute-start.3 = (f32[10,1,256]{2,1,0:T(1,128)S(1)}, f32[10,1,256]{2,1,0:T(1,128)S(1)}, u32[]{:S(2)}, u32[]{:S(2)}) collective-permute-start(f32[10,1,256]{2,1,0:T(1,128)S(1)} %get-tuple-element.27), channel_id=1, source_target_pairs={{0,1},{1,2},{2,3},{3,4},{4,5},{5,6},{6,7},{7,8},{8,9},{9,10},{10,1... | collective-permute-start | bytes 30728 | tf_op jit(solution)/shard_map/ppermute | solution.py:28
  26.6 6.8 collective-permute-start.4
  45.2 6.8 collective-permute-start.8
  63.8 6.8 collective-permute-start.12
  82.3 6.8 collective-permute-start.17
  105.4 6.5 collective-permute-start.21
  123.4 6.5 collective-permute-start.25
  141.4 6.5 collective-permute-start.29
  177.4 6.5 collective-permute-start.37
  284.0 7.4 %collective-permute-start.61 = (f32[1,4,32]{2,1,0:T(4,128)S(1)}, f32[1,4,32]{2,1,0:T(4,128)S(1)}, u32[]{:S(2)}, u32[]{:S(2)}) collective-permute-start(f32[1,4,32]{2,1,0:T(4,128)S(1)} %get-tuple-element.5), channel_id=1, source_target_pairs={{16,0},{32,16},{48,32},{64,48},{80,64},{96,80},{112,96},{128,112},... | collective-permute-start | bytes 1544 | tf_op jit(solution)/shard_map/ppermute | solution.py:29
  301.5 7.9 %collective-permute-start.65 = (f32[1,4,32]{2,1,0:T(4,128)S(1)}, f32[1,4,32]{2,1,0:T(4,128)S(1)}, u32[]{:S(2)}, u32[]{:S(2)}) collective-permute-start(f32[1,4,32]{2,1,0:T(4,128)S(1)} %fusion.818), channel_id=1, source_target_pairs={{16,0},{32,16},{48,32},{64,48},{80,64},{96,80},{112,96},{128,112},... | collective-permute-start | bytes 1544 | tf_op jit(solution)/shard_map/ppermute | solution.py:29
  303.5 6.7 collective-permute-start.64
  319.5 7.9 %collective-permute-start.69 = (f32[1,4,32]{2,1,0:T(4,128)S(1)}, f32[1,4,32]{2,1,0:T(4,128)S(1)}, u32[]{:S(2)}, u32[]{:S(2)}) collective-permute-start(f32[1,4,32]{2,1,0:T(4,128)S(1)} %fusion.786), channel_id=1, source_target_pairs={{16,0},{32,16},{48,32},{64,48},{80,64},{96,80},{112,96},{128,112},... | collective-permute-start | bytes 1544 | tf_op jit(solution)/shard_map/ppermute | solution.py:29
  321.4 6.7 collective-permute-start.68
  337.3 7.9 %collective-permute-start.73 = (f32[1,4,32]{2,1,0:T(4,128)S(1)}, f32[1,4,32]{2,1,0:T(4,128)S(1)}, u32[]{:S(2)}, u32[]{:S(2)}) collective-permute-start(f32[1,4,32]{2,1,0:T(4,128)S(1)} %fusion.754), channel_id=1, source_target_pairs={{16,0},{32,16},{48,32},{64,48},{80,64},{96,80},{112,96},{128,112},... | collective-permute-start | bytes 1544 | tf_op jit(solution)/shard_map/ppermute | solution.py:29
  339.2 6.7 collective-permute-start.72
  355.0 7.9 %collective-permute-start.77 = (f32[1,4,32]{2,1,0:T(4,128)S(1)}, f32[1,4,32]{2,1,0:T(4,128)S(1)}, u32[]{:S(2)}, u32[]{:S(2)}) collective-permute-start(f32[1,4,32]{2,1,0:T(4,128)S(1)} %fusion.722), channel_id=1, source_target_pairs={{16,0},{32,16},{48,32},{64,48},{80,64},{96,80},{112,96},{128,112},... | collective-permute-start | bytes 1544 | tf_op jit(solution)/shard_map/ppermute | solution.py:29
  357.0 6.7 collective-permute-start.76
  372.8 7.9 %collective-permute-start.81 = (f32[1,4,32]{2,1,0:T(4,128)S(1)}, f32[1,4,32]{2,1,0:T(4,128)S(1)}, u32[]{:S(2)}, u32[]{:S(2)}) collective-permute-start(f32[1,4,32]{2,1,0:T(4,128)S(1)} %fusion.690), channel_id=1, source_target_pairs={{16,0},{32,16},{48,32},{64,48},{80,64},{96,80},{112,96},{128,112},... | collective-permute-start | bytes 1544 | tf_op jit(solution)/shard_map/ppermute | solution.py:29
  374.7 6.7 collective-permute-start.80
  390.6 7.9 %collective-permute-start.85 = (f32[1,4,32]{2,1,0:T(4,128)S(1)}, f32[1,4,32]{2,1,0:T(4,128)S(1)}, u32[]{:S(2)}, u32[]{:S(2)}) collective-permute-start(f32[1,4,32]{2,1,0:T(4,128)S(1)} %fusion.658), channel_id=1, source_target_pairs={{16,0},{32,16},{48,32},{64,48},{80,64},{96,80},{112,96},{128,112},... | collective-permute-start | bytes 1544 | tf_op jit(solution)/shard_map/ppermute | solution.py:29
  392.5 6.7 collective-permute-start.84
  408.3 7.9 %collective-permute-start.89 = (f32[1,4,32]{2,1,0:T(4,128)S(1)}, f32[1,4,32]{2,1,0:T(4,128)S(1)}, u32[]{:S(2)}, u32[]{:S(2)}) collective-permute-start(f32[1,4,32]{2,1,0:T(4,128)S(1)} %fusion.626), channel_id=1, source_target_pairs={{16,0},{32,16},{48,32},{64,48},{80,64},{96,80},{112,96},{128,112},... | collective-permute-start | bytes 1544 | tf_op jit(solution)/shard_map/ppermute | solution.py:29
  410.3 6.7 collective-permute-start.88
  426.3 8.0 %collective-permute-start.92 = (f32[1,8,64]{2,1,0:T(8,128)S(1)}, f32[1,8,64]{2,1,0:T(8,128)S(1)}, u32[]{:S(2)}, u32[]{:S(2)}) collective-permute-start(f32[1,8,64]{2,1,0:T(8,128)S(1)} %get-tuple-element.145), channel_id=1, source_target_pairs={{0,16},{16,32},{32,48},{48,64},{64,80},{80,96},{96,112},{112,128},... | collective-permute-start | bytes 6152 | tf_op jit(solution)/shard_map/ppermute | solution.py:28
  522.0 6.5 collective-permute-start.113
  540.0 6.5 collective-permute-start.117
  613.0 6.8 collective-permute-start.132
  631.6 6.8 collective-permute-start.136
  650.2 6.8 collective-permute-start.140
  668.7 6.8 collective-permute-start.144
  (121 other events, 678.6 us)
where the time goes:
time: 690 us; the launch traced here: 686 us
  starting transfers between devices  407 us (59%)
  waiting for transfers between devices  256 us (37%)
  other arithmetic  12.5 us (2%)
  local copies, waits for them, and re-layouts  8.06 us (1%)
    ppermute x74, waiting for transfers between devices, extended_2(): after = lax.ppermute(leading, axis, down)  251 us
    ppermute x74, starting transfers between devices, extended_2(): before = lax.ppermute(last, axis, up)  225 us
    ppermute x74, starting transfers between devices, extended_2(): after = lax.ppermute(leading, axis, down)  182 us
  transfers between devices with their start and end apart: 148, of which 74 were waited for; matrix products, arithmetic and copies ran while one was open for 0% of the time, Pallas kernels for 0%

commit v1 on v0

v1 whole, which is shorter than its diff:
```python
import jax
import jax.numpy as jnp
from jax import lax
from jax.experimental import pallas as pl
from jax.experimental.pallas import tpu as pltpu
from jax.sharding import PartitionSpec as P

F32 = jnp.float32
RELAXATION = 0.8
KEEP = 1.0 - RELAXATION
N = 16
HI = lax.Precision.HIGHEST


def ring(value, axis, step):
    return lax.ppermute(value, axis, [(i, (i + step) % N) for i in range(N)])


def everyone(block, axis):
    copies = jnp.broadcast_to(block[None], (N,) + block.shape)
    return lax.all_to_all(copies, axis, 0, 0)


def iota(shape, dim):
    return lax.broadcasted_iota(jnp.int32, shape, dim)


def weight(fine, coarse):
    d = fine - 2 * coarse
    return jnp.where((d == 0) | (d == 1), 0.75, jnp.where((d == -1) | (d == 2), 0.25, 0.0))


def matrix(rows, lanes, entry):
    return entry(iota((rows, lanes), 0), iota((rows, lanes), 1)).astype(F32)


def dot(a, b):
    return jnp.dot(a, b, precision=HI, preferred_element_type=F32)


def batch(lo, hi, group, compute, store):
    def some(indices):
        for i, value in [(i, compute(i)) for i in indices]:
            store(i, value)

    count = (hi - lo) // group
    if count == 1:
        some(range(lo, lo + group))
    elif count > 1:
        lax.fori_loop(
            0, count, lambda n, c: (some([lo + n * group + i for i in range(group)]), c)[1], 0
        )
    if lo + count * group < hi:
        some(range(lo + count * group, hi))


def put(ref):
    def store(i, value):
        ref[i] = value

    return store


def rows_valid(shape, first, count):
    row = iota(shape, 0) + first
    return (row >= 0) & (row < count)


def between(i, count):
    return (i >= 0) & (i < count)


def z_shifts(c, period):
    lane = iota(c.shape, 1) & (period - 1)
    size = c.shape[1]
    below = jnp.where(lane > 0, pltpu.roll(c, 1, 1), 0.0)
    above = jnp.where(lane < period - 1, pltpu.roll(c, size - 1, 1), 0.0)
    return below, above


def grow_rows(coarse, ref, index, count):
    mid = 0.75 * coarse[4 : 4 + count]
    ref[index, pl.ds(0, count, stride=2), :] = mid + 0.25 * coarse[3 : 3 + count]
    ref[index, pl.ds(1, count, stride=2), :] = mid + 0.25 * coarse[5 : 5 + count]


def halve_rows(ref, index, count):
    part = [ref[index, pl.ds(7 + i, count, stride=2), :] for i in range(4)]
    return 0.25 * (part[0] + part[3]) + 0.75 * (part[1] + part[2])


def six(before, c, after):
    rows = c.shape[0]
    below, above = z_shifts(c, c.shape[1])
    return before + after + pltpu.roll(c, 1, 0) + pltpu.roll(c, rows - 1, 0) + below + above


def fine_down(
    pos, source, damping, xlo, xhi, ylo, yhi, v_out, g_out, s_out, w_out, a, b, s, w, t
):
    ix, iy = pos[0], pos[1]
    row_ok = rows_valid((48, 256), iy * 32 - 8, 512)

    def start(lo, hi, s_mid, d_mid):
        def compute(p):
            ok = row_ok & between(ix * 8 + p - 7, 128)
            rows = jnp.concatenate([ylo[0, p], s_mid(p - lo), yhi[0, p]], axis=0)
            damp = jnp.concatenate([ylo[1, p], d_mid(p - lo), yhi[1, p]], axis=0)
            return rows, jnp.where(ok, RELAXATION / (6.0 + damp), 0.0)

        def store(p, value):
            s[p], w[p] = value
            a[p] = value[0] * value[1]

        batch(lo, hi, 1, compute, store)

    start(0, 7, lambda i: xlo[0, i], lambda i: xlo[1, i])
    start(7, 15, lambda i: source[i], lambda i: damping[i])
    start(15, 22, lambda i: xhi[0, i], lambda i: xhi[1, i])

    def sweep(src, dst, lo, hi, off):
        def compute(p):
            c = src[p]
            return KEEP * c + w[p] * (s[p] + six(src[p - 1], c, src[p + 1]))

        def store(p, value):
            dst[p - off] = value

        batch(lo, hi, 2, compute, store)

    sweep(a, b, 1, 21, 0)
    sweep(b, a, 2, 20, 0)
    sweep(a, v_out, 3, 19, 3)

    def residual(mid, first):
        def compute(p):
            ok = row_ok & between(ix * 8 + p - 7, 128)
            damp = jnp.concatenate([ylo[1, p], mid(p - first), yhi[1, p]], axis=0)
            c = v_out[p - 3]
            r = s[p] + six(v_out[p - 4], c, v_out[p - 2]) - (6.0 + damp) * c
            return jnp.where(ok, r, 0.0)

        return compute

    batch(4, 7, 3, residual(lambda i: xlo[1, i], 0), put(b))
    batch(7, 15, 2, residual(lambda i: damping[i], 7), put(b))
    batch(15, 18, 3, residual(lambda i: xhi[1, i], 15), put(b))
    s_out[...] = s[3:19]
    w_out[...] = w[3:19]

    rz = matrix(256, 128, weight)

    def coarse(j):
        q = 2 * j + 4
        return dot(0.25 * (b[q] + b[q + 3]) + 0.75 * (b[q + 1] + b[q + 2]), rz)

    batch(0, 6, 6, coarse, put(t))
    batch(0, 6, 6, lambda j: halve_rows(t, j, 16), put(g_out))


def fine_up(pos, s, w, v_in, c1, out, a, b, u):
    ix, iy = pos[0], pos[1]
    row_ok = rows_valid((48, 256), iy * 32 - 8, 512)
    coarse_ok = rows_valid((32, 128), iy * 16 - 8, 256)
    for q in range(10):
        ok = coarse_ok & between(ix * 4 + q - 3, 64)
        grow_rows(jnp.where(ok, c1[q], 0.0), u, q, 24)

    pz = matrix(128, 256, lambda j, f: weight(f, j))

    def add(f):
        ok = row_ok & between(ix * 8 + f - 4, 128)
        h = f // 2
        fine = dot(0.75 * u[h + 1] + 0.25 * u[h + 2 * (f % 2)], pz)
        return v_in[f] + jnp.where(ok, fine, 0.0)

    for h in range(0, 16, 4):
        batch(h, h + 4, 4, add, put(a))

    def sweep(src, dst, lo, hi, keep_rows):
        def compute(p):
            c = src[p]
            return KEEP * c + w[p] * (s[p] + six(src[p - 1], c, src[p + 1]))

        def store(p, value):
            if keep_rows:
                dst[p - lo] = value[8:40]
            else:
                dst[p] = value

        batch(lo, hi, 2, compute, store)

    sweep(a, b, 1, 15, False)
    sweep(b, a, 2, 14, False)
    sweep(a, b, 3, 13, False)
    sweep(b, out, 4, 12, True)


def one_coefficient(cx, clo, chi, k, p):
    return jnp.concatenate([clo[k, p], cx[k, p], chi[k, p]], axis=0)


def one_weights(w, cx, clo, chi, ix, iy):
    def compute(p):
        ok = rows_valid((32, 128), iy * 16 - 8, 256) & between(ix * 4 + p - 4, 64)
        return jnp.where(ok, RELAXATION / one_coefficient(cx, clo, chi, 13, p), 0.0)

    batch(0, 12, 4, compute, put(w))


def one_spread(v, vz, lo, hi):
    def compute(p):
        c = v[p]
        below, above = z_shifts(c, 128)
        return below, c, above

    def store(p, value):
        for i in range(3):
            vz[i, p] = value[i]

    batch(lo, hi, 4, compute, store)


def one_others(vz, cx, clo, chi, p, cp):
    parts = []
    for a in range(3):
        total = None
        for c in range(3):
            plane = vz[c, p + a - 1]
            for b in range(3):
                k = 9 * a + 3 * b + c
                if k == 13:
                    continue
                moved = plane if b == 1 else pltpu.roll(plane, 1 if b == 0 else 31, 0)
                term = one_coefficient(cx, clo, chi, k, cp) * moved
                total = term if total is None else total + term
        parts.append(total)
    return parts[0] + parts[1] + parts[2]


def one_down(pos, g, cx, clo, chi, g_out, v_out, v, vz, w, t):
    ix, iy = pos[0], pos[1]
    one_weights(w, cx, clo, chi, ix, iy)
    row_ok = rows_valid((32, 128), iy * 16 - 8, 256)
    for p in (0, 13):
        v[p] = jnp.where(row_ok & between(ix * 4 + p - 5, 64), g[p], 0.0)
    batch(1, 13, 4, lambda p: w[p - 1] * g[p], put(v))

    def update(p):
        rest = one_others(vz, cx, clo, chi, p, p - 1)
        return KEEP * v[p] + w[p - 1] * (g[p] - rest)

    for k in range(3):
        one_spread(v, vz, k, 14 - k)
        batch(1 + k, 13 - k, 2, update, put(v))
    one_spread(v, vz, 3, 11)

    def residual(p):
        ok = row_ok & between(ix * 4 + p - 5, 64)
        rest = one_others(vz, cx, clo, chi, p, p - 1)
        own = one_coefficient(cx, clo, chi, 13, p - 1) * vz[1, p]
        return jnp.where(ok, g[p] - own - rest, 0.0)

    batch(4, 10, 2, residual, put(v))
    for p in range(4):
        v_out[p] = vz[1, p + 5, 8:24]
    total = None
    for j in range(2):
        q = 2 * j + 4
        t[j] = 0.25 * (v[q] + v[q + 3]) + 0.75 * (v[q + 1] + v[q + 2])
    for j in range(2):
        rz = matrix(128, 128, lambda f, m: jnp.where(m >> 6 == j, weight(f, m & 63), 0.0))
        term = dot(halve_rows(t, j, 8), rz)
        total = term if total is None else total + term
    g_out[...] = total


def two_coefficient(c2, block, k):
    ref, index = c2[block]
    parts = []
    for j in range(3):
        rows = pl.ds((j * 27 + k) * 8, 8)
        parts.append(ref[rows, :] if index is None else ref[index, rows, :])
    return jnp.concatenate(parts, axis=0)


def two_blocks(far_lo, before, own, after, far_hi):
    return [(far_lo, 0), (far_lo, 1), (before, None), (own, None), (after, None)] + [
        (far_hi, 0),
        (far_hi, 1),
    ]


def two_weights(w, c2, ix, iy):
    row_ok = rows_valid((24, 128), iy * 8 - 8, 128)

    def compute(b):
        ok = row_ok & between(ix + b - 3, 16)
        return jnp.where(ok, RELAXATION / two_coefficient(c2, b, 13), 0.0)

    batch(0, 7, 7, compute, put(w))


def two_spread(v, vx, lo, hi):
    low = iota((24, 128), 1) < 64
    turned = {b: pltpu.roll(v[b], 64, 1) for b in range(lo - 1, hi + 1)}
    for b in range(lo, hi):
        moved = (
            jnp.where(low, turned[b - 1], turned[b]),
            v[b],
            jnp.where(low, turned[b], turned[b + 1]),
        )
        for a, c in enumerate(moved):
            vx[3 * a, b], vx[3 * a + 2, b] = z_shifts(c, 64)
            vx[3 * a + 1, b] = c


def two_others(vx, c2, b):
    parts = []
    for a in range(3):
        total = None
        for c in range(3):
            plane = vx[3 * a + c, b]
            for s in range(3):
                k = 9 * a + 3 * s + c
                if k == 13:
                    continue
                moved = plane if s == 1 else pltpu.roll(plane, 1 if s == 0 else 23, 0)
                term = two_coefficient(c2, b - 1, k) * moved
                total = term if total is None else total + term
        parts.append(total)
    return parts[0] + parts[1] + parts[2]


def two_sweep(v, vx, w, g, c2, lo, hi):
    two_spread(v, vx, lo, hi)

    def compute(b):
        return KEEP * v[b] + w[b - 1] * (g[b - 1] - two_others(vx, c2, b))

    batch(lo, hi, hi - lo, compute, put(v))


def twice(step):
    lax.fori_loop(0, 2, lambda _, c: (step(), c)[1], 0)


def two_sources(g, own, ix):
    batch(0, 7, 7, lambda b: g[jnp.clip(ix + b - 3, 0, 15)], put(own))


def two_down(
    pos, g_all, far_lo, before, own, after, far_hi, g_out, v_out, v, vx, w, g, t
):
    ix, iy = pos[0], pos[1]
    c2 = two_blocks(far_lo, before, own, after, far_hi)
    two_weights(w, c2, ix, iy)
    two_sources(g_all, g, ix)
    for b in (0, 8):
        v[b] = jnp.zeros((24, 128), F32)
    batch(1, 8, 7, lambda b: w[b - 1] * g[b - 1], put(v))
    twice(lambda: two_sweep(v, vx, w, g, c2, 2, 7))
    two_sweep(v, vx, w, g, c2, 3, 6)
    two_spread(v, vx, 3, 6)
    v_out[...] = v[4, 8:16]
    row_ok = rows_valid((24, 128), iy * 8 - 8, 128)

    def residual(b):
        rest = two_coefficient(c2, b - 1, 13) * v[b] + two_others(vx, c2, b)
        return jnp.where(row_ok & between(ix + b - 4, 16), g[b - 1] - rest, 0.0)

    batch(3, 6, 3, residual, put(v))
    low = iota((24, 128), 1) < 64
    here = 0.75 * v[4] + 0.25 * jnp.where(low, v[5], v[3])
    t[0] = dot(here, matrix(128, 128, lambda f, m: weight(f & 63, m & 31)))
    y = halve_rows(t, 0, 4)
    y = jnp.where(iota((4, 128), 1) >> 5 == iota((4, 128), 0), y, 0.0)
    g_out[...] = jnp.broadcast_to(jnp.sum(y, axis=0, keepdims=True), (8, 128))


def three_y(c):
    lane = iota(c.shape, 1)
    rows = c.shape[0]
    down = pltpu.roll(c, 32, 1)
    below = jnp.where(lane >= 32, down, pltpu.roll(down, 1, 0))
    up = pltpu.roll(c, 96, 1)
    above = jnp.where(lane < 96, up, pltpu.roll(up, rows - 1, 0))
    return below, above


def three_solve(v, vx, w, g, c3, iy):
    yb = iota((8, 128), 0)
    ok = (yb + iy >= 3) & (yb + iy < 19) & (yb < 7)

    def coefficient(x, k):
        return c3[x, pl.ds(k * 8, 8), :]

    for x in (0, 17):
        v[x] = jnp.zeros((8, 128), F32)
        for k in range(9):
            vx[k, x] = jnp.zeros((8, 128), F32)
    batch(
        0, 16, 16, lambda x: jnp.where(ok, RELAXATION / coefficient(x, 13), 0.0), put(w)
    )
    for x in range(16):
        v[x + 1] = w[x] * g[x, 0:8]

    def spread(x):
        c = v[x]
        below, above = three_y(c)
        values = []
        for plane in (below, c, above):
            left, right = z_shifts(plane, 32)
            values += [left, plane, right]
        return values

    def keep(x, values):
        for k in range(9):
            vx[k, x] = values[k]

    def update(x):
        parts = []
        for a in range(3):
            part = None
            for m in range(9):
                k = 9 * a + m
                if k == 13:
                    continue
                term = coefficient(x - 1, k) * vx[m, x + a - 1]
                part = term if part is None else part + term
            parts.append(part)
        rest = parts[0] + parts[1] + parts[2]
        return KEEP * v[x] + w[x - 1] * (g[x - 1, 0:8] - rest)

    def sweep(_, carry):
        for x in (1, 5, 9, 13):
            batch(x, x + 4, 4, spread, keep)
        for x in (1, 5, 9, 13):
            batch(x, x + 4, 4, update, put(v))
        return carry

    lax.fori_loop(0, 7, sweep, 0)


def coarse_up(
    pos, gv, c3, g2_all, far_lo, before, own, after, far_hi, g1, v1, v1lo, v1hi,
    cx, clo, chi, out,
    s3, vx3, w3, e, d, pc, s2, vx2, w2, g2, u, s1, vz, w1,
):
    ix, iy = pos[0], pos[1]
    c2 = two_blocks(far_lo, before, own, after, far_hi)
    three_solve(s3, vx3, w3, gv, c3, iy)
    two_weights(w2, c2, ix, iy)
    two_sources(g2_all, g2, ix)
    one_weights(w1, cx, clo, chi, ix, iy)
    for j in range(9):
        x = jnp.clip(ix + j - 4, 0, 15)
        mid = 0.75 * s3[x + 1]
        for p in range(2):
            c = mid + 0.25 * s3[x + 2 * p]
            below, above = three_y(c)
            e[0, j, :, p * 128 : p * 128 + 128] = 0.75 * c + 0.25 * below
            e[1, j, :, p * 128 : p * 128 + 128] = 0.75 * c + 0.25 * above
    for q in range(4):

        def entry(r, m):
            same = (r >> 7 == m >> 6) & ((r >> 5) & 3 == q)
            return jnp.where(same, weight(m & 63, r & 31), 0.0)

        pz2 = matrix(256, 128, entry)
        for s in range(2):
            d[4 * s + q] = dot(e[s].reshape(72, 256), pz2).reshape(9, 8, 128)
    for s in range(2):
        for q in range(4):
            for j in range(9):
                pc[j, pl.ds(2 * q + s, 8, stride=8), :] = d[4 * s + q, j]
    row_two = rows_valid((24, 128), iy * 8 - 8, 128)
    for j in range(9):
        ok = row_two & between(ix + j - 4, 16)
        held = gv[jnp.clip(ix + j - 4, 0, 15), 8:32]
        s2[j] = jnp.where(ok, held + pc[j, 16:40], 0.0)
    for lo, hi in ((1, 8), (2, 7)):
        twice(lambda: two_sweep(s2, vx2, w2, g2, c2, lo, hi))
    low = iota((24, 128), 1) < 64
    for k in range(3):
        lo, here, hi = s2[k + 2], s2[k + 3], s2[k + 4]
        grow_rows(jnp.where(low, 0.75 * here, 0.25 * lo), u, 4 * k, 16)
        grow_rows(jnp.where(low, 0.75, 0.25) * here, u, 4 * k + 1, 16)
        grow_rows(jnp.where(low, 0.25, 0.75) * here, u, 4 * k + 2, 16)
        grow_rows(jnp.where(low, 0.25 * hi, 0.75 * here), u, 4 * k + 3, 16)
    row_one = rows_valid((32, 128), iy * 16 - 8, 256)
    pz1 = matrix(128, 128, lambda r, f: weight(f, r & 63))

    def add(p):
        ok = row_one & between(ix * 4 + p - 4, 64)
        held = jnp.concatenate([v1lo[p], v1[p], v1hi[p]], axis=0)
        return jnp.where(ok, held + dot(u[p], pz1), 0.0)

    for p in (0, 4, 8):
        batch(p, p + 4, 4, add, put(s1))

    def update(p):
        rest = one_others(vz, cx, clo, chi, p, p)
        return KEEP * s1[p] + w1[p] * (g1[p + 1] - rest)

    for k in range(4):
        one_spread(s1, vz, k, 12 - k)
        batch(1 + k, 11 - k, 2, update, put(s1))
    for p in range(4):
        out[p] = s1[p + 4, 8:24]


def vm(*shape):
    return pltpu.VMEM(shape, F32)


def call(kernel, name, outs, scratch, pos, *operands):
    shapes = [jax.ShapeDtypeStruct(s, F32) for s in outs]
    return pl.pallas_call(
        kernel,
        name=name,
        out_shape=shapes,
        in_specs=[pl.BlockSpec(memory_space=pltpu.SMEM)]
        + [pl.BlockSpec(memory_space=pltpu.VMEM)] * len(operands),
        out_specs=[pl.BlockSpec(memory_space=pltpu.VMEM)] * len(outs),
        scratch_shapes=scratch,
        compiler_params=pltpu.CompilerParams(vmem_limit_bytes=50 * 2**20),
    )(pos, *operands)


def both(value, axis, dim, width):
    length = value.shape[dim]
    last = lax.slice_in_dim(value, length - width, length, axis=dim)
    first = lax.slice_in_dim(value, 0, width, axis=dim)
    return ring(last, axis, 1), ring(first, axis, -1)


def wide(value, axis, dim, width):
    before, after = both(value, axis, dim, width)
    return jnp.concatenate([before, value, after], axis=dim)


def after_all(value, *others):
    return lax.optimization_barrier((value,) + others)[0]


def on_device(source, damping, coarse_one, coarse_two, coarse_three):
    pos = jnp.stack([lax.axis_index("gx"), lax.axis_index("gy")]).astype(jnp.int32)

    with jax.named_scope("fine_halo"):
        last = jnp.stack([source[1:], damping[1:]])
        first = jnp.stack([source[:7], damping[:7]])
        xlo, xhi = ring(last, "gx", 1), ring(first, "gx", -1)

    with jax.named_scope("two_three_halo"):
        coarse_two, coarse_three, one = lax.optimization_barrier(
            (coarse_two, coarse_three, coarse_one, last, first)
        )[:3]
        c2 = jnp.concatenate([coarse_two[:, 0], coarse_two[:, 1]], axis=-1)
        c3 = jnp.concatenate([coarse_three[:, 0, i] for i in range(4)], axis=-1)
        c3 = jnp.pad(c3, ((0, 5), (0, 0)))
        own = jnp.concatenate([c2.reshape(216, 128), c3], axis=0)
        before, after = ring(own, "gy", 1), ring(own, "gy", -1)
        two = jnp.concatenate([before[:216], own[:216], after[:216]])
        three = jnp.stack([before[216:], c3, after[216:]])
        far_before, far_after = ring(three, "gy", 2), ring(three, "gy", -2)
        seven = jnp.concatenate([far_before[:2], three, far_after[1:], c3[None]])
        seven = jnp.transpose(seven[:, :27], (1, 0, 2)).reshape(216, 128)
        c3 = lax.all_gather(seven, "gx")
        one_lo, one_hi = both(one, "gy", 2, 8)

    with jax.named_scope("fine_halo"):
        edge = []
        for rows in (slice(24, 32), slice(0, 8)):
            mid = jnp.stack([source[:, rows], damping[:, rows]])
            edge.append(jnp.concatenate([xlo[:, :, rows], mid, xhi[:, :, rows]], axis=1))
        ylo, yhi = ring(edge[0], "gy", 1), ring(edge[1], "gy", -1)

    with jax.named_scope("one_halo"):
        cxlo, cxhi = both(after_all(coarse_one, *edge), "gx", 1, 4)

    with jax.named_scope("fine_down"):
        v0, g1, s0, w0 = call(
            fine_down, "fine_down",
            [(16, 48, 256), (6, 16, 128), (16, 48, 256), (16, 48, 256)],
            [vm(22, 48, 256)] * 4 + [vm(6, 48, 128)],
            pos, source, damping, xlo, xhi, ylo, yhi,
        )

    with jax.named_scope("one_halo"):
        cxlo, cxhi, g1 = lax.optimization_barrier((cxlo, cxhi, g1))
        sides = jnp.concatenate([cxlo, cxhi], axis=1)
        side_lo, side_hi = both(sides, "gy", 2, 8)
        cx = jnp.concatenate([cxlo, coarse_one, cxhi], axis=1)

    with jax.named_scope("one_exchange"):
        edge_lo = RELAXATION * g1[0:1] / cxlo[13, 3:4]
        edge_hi = RELAXATION * g1[5:6] / cxhi[13, 0:1]
        up = jnp.concatenate([edge_lo, g1[1:5]])
        down = jnp.concatenate([g1[1:5], edge_hi])
        before, after = ring(up, "gx", 1), ring(down, "gx", -1)
        g1e = wide(jnp.concatenate([before, g1[1:5], after]), "gy", 1, 8)

    with jax.named_scope("two_halo"):
        two = after_all(two, up, down)
        tlo, thi = ring(two, "gx", 1), ring(two, "gx", -1)
        above, below = jnp.stack([two, thi]), jnp.stack([tlo, two])
        far_lo, far_hi = ring(above, "gx", 3), ring(below, "gx", -3)
        blocks = (far_lo, tlo, two, thi, far_hi)

    with jax.named_scope("one_down"):
        g1e = after_all(g1e, above, below)
        clo = jnp.concatenate([side_lo[:, :4], one_lo, side_lo[:, 4:]], axis=1)
        chi = jnp.concatenate([side_hi[:, :4], one_hi, side_hi[:, 4:]], axis=1)
        g2, v1 = call(
            one_down, "one_down", [(8, 128), (4, 16, 128)],
            [vm(14, 32, 128), vm(3, 14, 32, 128), vm(12, 32, 128), vm(2, 32, 128)],
            pos, g1e, cx, clo, chi,
        )

    with jax.named_scope("two_exchange"):
        g2e = everyone(wide(g2, "gy", 0, 8), "gx")

    with jax.named_scope("one_values"):
        v1 = wide(v1, "gx", 0, 4)

    with jax.named_scope("two_down"):
        g3, v2 = call(
            two_down, "two_down", [(8, 128), (8, 128)],
            [
                vm(9, 24, 128), vm(9, 9, 24, 128), vm(7, 24, 128), vm(7, 24, 128),
                vm(1, 24, 128),
            ],
            pos, g2e, *blocks,
        )

    with jax.named_scope("three_exchange"):
        up = jnp.concatenate([g3, v2, v1[:, 8:].reshape(96, 128)])
        down = jnp.concatenate([g3, v2, v1[:, :8].reshape(96, 128)])
        before, after = ring(up, "gy", 1), ring(down, "gy", -1)
        v1lo, v1hi = before[16:].reshape(12, 8, 128), after[16:].reshape(12, 8, 128)
        trip = jnp.concatenate([before[:1], g3[:1], after[:1]])
        far_before, far_after = ring(trip, "gy", 2), ring(trip, "gy", -2)
        gv = everyone(
            jnp.concatenate(
                [far_before[:2], trip, far_after[1:], g3[:1], before[8:16], v2, after[8:16]]
            ),
            "gx",
        )

    with jax.named_scope("coarse_up"):
        (c1,) = call(
            coarse_up, "coarse_up", [(4, 16, 128)],
            [
                vm(18, 8, 128), vm(9, 18, 8, 128), vm(16, 8, 128), vm(2, 9, 8, 256),
                vm(8, 9, 8, 128), vm(9, 64, 128),
                vm(9, 24, 128), vm(9, 9, 24, 128), vm(7, 24, 128), vm(7, 24, 128),
                vm(12, 32, 128), vm(12, 32, 128), vm(3, 12, 32, 128), vm(12, 32, 128),
            ],
            pos, gv, c3, g2e, *blocks, g1e, v1, v1lo, v1hi, cx, clo, chi,
        )

    with jax.named_scope("one_back"):
        c1e = wide(wide(c1, "gx", 0, 3), "gy", 1, 8)

    with jax.named_scope("fine_up"):
        (out,) = call(
            fine_up, "fine_up", [(8, 32, 256)],
            [vm(16, 48, 256)] * 2 + [vm(10, 48, 128)], pos, s0, w0, v0, c1e,
        )
    return out


def solution(mesh):
    in_specs = (
        P("gx", "gy", None),
        P("gx", "gy", None),
        P(None, "gx", "gy", None),
        P(None, "gx", "gy", None),
        P(None, "gx", "gy", None),
    )
    return jax.shard_map(
        on_device, mesh=mesh, in_specs=in_specs, out_specs=P("gx", "gy", None), check_vma=False
    )
```

time: 690 us -> 193 us (0.28)
  the two profiles are of different devices: /device:TPU:103 before, /device:TPU:0 now
where the time goes in v1:
time: 193 us
  waiting for transfers between devices  68.8 us (36%)
  starting transfers between devices  64.6 us (33%)
  Pallas kernels  30.6 us (16%)
  between operations  14 us (7%)
  local copies, waits for them, and re-layouts  10 us (5%)
  other arithmetic  4.9 us (3%)
    ppermute x34, waiting for transfers between devices, ring(): return lax.ppermute(value, axis, [(i, (i + step) % N) for i in range(N)])  58.5 us
    ppermute x34, starting transfers between devices, ring(): return lax.ppermute(value, axis, [(i, (i + step) % N) for i in range(N)])  54.4 us
    pallas_call x5, Pallas kernels, call(): pl.pallas_call(kernel, name=name, out_shape=shapes, in_specs=[pl.BlockSpe...  30.6 us
    all_to_all x2, waiting for transfers between devices, everyone(): return lax.all_to_all(copies, axis, 0, 0)  10.3 us
    all_to_all x2, starting transfers between devices, everyone(): return lax.all_to_all(copies, axis, 0, 0)  10.2 us
    unnamed x49, local copies, waits for them, and re-layouts  4.49 us
  transfers between devices with their start and end apart: 37, of which 19 were waited for; matrix products, arithmetic and copies ran while one was open for 6% of the time, Pallas kernels for 8%

profile of v1, /device:TPU:0, one launch (start us, length us, event | category | flops | bytes accessed | tf_op | source)
XLA Modules:
  0.0 192.9 jit_solution(1101894477763063119)
XLA Ops:
  8.9 5.3 %collective-permute-start.1 = (f32[2,7,32,256]{3,2,1,0:T(8,128)}, f32[2,7,32,256]{3,2,1,0:T(8,128)S(1)}, u32[]{:S(2)}, u32[]{:S(2)}) collective-permute-start(f32[2,7,32,256]{3,2,1,0:T(8,128)} %pad_maximum_fusion.5), channel_id=1, source_target_pairs={{0,240},{16,0},{32,16},{48,32},{64,48},{80,64},{96,80},{112,96},{1... | collective-permute-start | bytes 1376264 | tf_op jit(solution)/shard_map/fine_halo/ppermute | solution.py:16
  14.5 3.2 %collective-permute-start.11 = (f32[248,128]{1,0:T(8,128)S(1)}, f32[248,128]{1,0:T(8,128)S(1)}, u32[]{:S(2)}, u32[]{:S(2)}) collective-permute-start(f32[248,128]{1,0:T(8,128)S(1)} %pad_maximum_fusion.11), channel_id=1, source_target_pairs={{0,15},{1,0},{2,1},{3,2},{4,3},{5,4},{6,5},{7,6},{8,7},{9,8},{10,9... | collective-permute-start | bytes 380936 | tf_op jit(solution)/shard_map/two_three_halo/ppermute | solution.py:16
  17.7 2.4 %collective-permute-done.11 = f32[248,128]{1,0:T(8,128)S(1)} collective-permute-done((f32[248,128]{1,0:T(8,128)S(1)}, f32[248,128]{1,0:T(8,128)S(1)}, u32[]{:S(2)}, u32[]{:S(2)}) %collective-permute-start.11) | collective-permute-done | bytes 127008 | tf_op jit(solution)/shard_map/two_three_halo/ppermute | solution.py:16
  20.2 3.1 %collective-permute-done.10 = f32[248,128]{1,0:T(8,128)S(1)} collective-permute-done((f32[248,128]{1,0:T(8,128)S(1)}, f32[248,128]{1,0:T(8,128)S(1)}, u32[]{:S(2)}, u32[]{:S(2)}) %collective-permute-start.10) | collective-permute-done | bytes 127008 | tf_op jit(solution)/shard_map/two_three_halo/ppermute | solution.py:16
  23.4 3.2 %collective-permute-start.29 = (f32[3,32,128]{2,1,0:T(8,128)S(1)}, f32[3,32,128]{2,1,0:T(8,128)S(1)}, u32[]{:S(2)}, u32[]{:S(2)}) collective-permute-start(f32[3,32,128]{2,1,0:T(8,128)S(1)} %pad_maximum_fusion.16), channel_id=1, source_target_pairs={{0,14},{1,15},{2,0},{3,1},{4,2},{5,3},{6,4},{7,5},{8,6},{9,7},{10,... | collective-permute-start | bytes 147464 | tf_op jit(solution)/shard_map/two_three_halo/ppermute | solution.py:16
  26.6 2.0 %collective-permute-done.28 = f32[3,32,128]{2,1,0:T(8,128)S(1)} collective-permute-done((f32[3,32,128]{2,1,0:T(8,128)S(1)}, f32[3,32,128]{2,1,0:T(8,128)S(1)}, u32[]{:S(2)}, u32[]{:S(2)}) %collective-permute-start.28) | collective-permute-done | bytes 49184 | tf_op jit(solution)/shard_map/two_three_halo/ppermute | solution.py:16
  30.3 5.3 %collective-permute-start.5 = (f32[27,4,16,128]{3,2,1,0:T(8,128)S(1)}, f32[27,4,16,128]{3,2,1,0:T(8,128)}, u32[]{:S(2)}, u32[]{:S(2)}) collective-permute-start(f32[27,4,16,128]{3,2,1,0:T(8,128)S(1)} %copy-done.13), channel_id=1, source_target_pairs={{0,240},{16,0},{32,16},{48,32},{64,48},{80,64},{96,80},{112,96},{1... | collective-permute-start | bytes 2654216 | tf_op jit(solution)/shard_map/one_halo/ppermute | solution.py:16
  35.7 2.9 %collective-permute-start.3 = (f32[2,22,8,256]{3,2,1,0:T(8,128)}, f32[2,22,8,256]{3,2,1,0:T(8,128)S(1)}, u32[]{:S(2)}, u32[]{:S(2)}) collective-permute-start(f32[2,22,8,256]{3,2,1,0:T(8,128)} %pad_maximum_fusion.7), channel_id=1, source_target_pairs={{0,15},{1,0},{2,1},{3,2},{4,3},{5,4},{6,5},{7,6},{8,7},{9,8},{10,9... | collective-permute-start | bytes 1081352 | tf_op jit(solution)/shard_map/fine_halo/ppermute | solution.py:16
  39.4 4.6 %collective-permute-done.2.ylo = f32[2,22,8,256]{3,2,1,0:T(8,128)S(1)} collective-permute-done((f32[2,22,8,256]{3,2,1,0:T(8,128)}, f32[2,22,8,256]{3,2,1,0:T(8,128)S(1)}, u32[]{:S(2)}, u32[]{:S(2)}) %collective-permute-start.2) | collective-permute-done | bytes 360480 | tf_op jit(solution)/shard_map/fine_halo/ppermute | solution.py:16
  43.9 6.6 %fine_down.1 = (f32[16,48,256]{2,1,0:T(8,128)S(1)}, f32[6,16,128]{2,1,0:T(8,128)S(1)}, f32[16,48,256]{2,1,0:T(8,128)S(1)}, f32[16,48,256]{2,1,0:T(8,128)}) custom-call(s32[2]{0:T(128)S(1)} %pad_add_fusion.pos, f32[8,32,256]{2,1,0:T(8,128)S(1)} %copy-done.5, f32[8,32,256]{2,1,0:T(8,128)S(1)} %copy-done.6, f32[2,7,32,256]{3,2,1,0:T(8,128)S(1)} %collective-permute-done.xlo, ...), custom_call_target="tpu_custom_call" | custom-call | tf_op jit(solution)/shard_map/fine_down/fine_down/pallas_call | solution.py:519
  50.5 1.9 collective-permute-done.4
  54.5 5.4 %collective-permute-start.7 = (f32[5,16,128]{2,1,0:T(8,128)S(1)}, f32[5,16,128]{2,1,0:T(8,128)S(1)}, u32[]{:S(2)}, u32[]{:S(2)}) collective-permute-start(f32[5,16,128]{2,1,0:T(8,128)S(1)} %get-tuple-element.82), channel_id=1, source_target_pairs={{0,240},{16,0},{32,16},{48,32},{64,48},{80,64},{96,80},{112,96},{1... | collective-permute-start | bytes 122888 | tf_op jit(solution)/shard_map/one_exchange/ppermute | solution.py:16
  62.9 4.4 %collective-permute-done.6 = f32[5,16,128]{2,1,0:T(8,128)S(1)} collective-permute-done((f32[5,16,128]{2,1,0:T(8,128)S(1)}, f32[5,16,128]{2,1,0:T(8,128)S(1)}, u32[]{:S(2)}, u32[]{:S(2)}) %collective-permute-start.6) | collective-permute-done | bytes 40992 | tf_op jit(solution)/shard_map/one_exchange/ppermute | solution.py:16
  67.5 5.3 %collective-permute-start.12 = (f32[648,128]{1,0:T(8,128)S(1)}, f32[648,128]{1,0:T(8,128)S(1)}, u32[]{:S(2)}, u32[]{:S(2)}) collective-permute-start(f32[648,128]{1,0:T(8,128)S(1)} %pad_maximum_fusion.8.own), channel_id=1, source_target_pairs={{0,240},{16,0},{32,16},{48,32},{64,48},{80,64},{96,80},{112,96},{1... | collective-permute-start | bytes 995336 | tf_op jit(solution)/shard_map/two_halo/ppermute | solution.py:16
  72.8 2.0 %collective-permute-start.16 = (f32[27,8,8,128]{3,2,1,0:T(8,128)S(1)}, f32[27,8,8,128]{3,2,1,0:T(8,128)S(1)}, u32[]{:S(2)}, u32[]{:S(2)}) collective-permute-start(f32[27,8,8,128]{3,2,1,0:T(8,128)S(1)} %get-tuple-element.39), channel_id=1, source_target_pairs={{0,15},{1,0},{2,1},{3,2},{4,3},{5,4},{6,5},{7,6},{8,7},{9,8},{10,9... | collective-permute-start | bytes 2654216 | tf_op jit(solution)/shard_map/one_halo/ppermute | solution.py:16
  74.9 4.7 %collective-permute-done.8 = f32[14,8,128]{2,1,0:T(8,128)S(1)} collective-permute-done((f32[14,8,128]{2,1,0:T(8,128)S(1)}, f32[14,8,128]{2,1,0:T(8,128)S(1)}, u32[]{:S(2)}, u32[]{:S(2)}) %collective-permute-start.8) | collective-permute-done | bytes 57376 | tf_op jit(solution)/shard_map/one_exchange/ppermute | solution.py:16
  79.7 8.0 %collective-permute-done.13.before = f32[648,128]{1,0:T(8,128)S(1)} collective-permute-done((f32[648,128]{1,0:T(8,128)S(1)}, f32[648,128]{1,0:T(8,128)S(1)}, u32[]{:S(2)}, u32[]{:S(2)}) %collective-permute-start.13) | collective-permute-done | bytes 331808 | tf_op jit(solution)/shard_map/two_halo/ppermute | solution.py:16
  90.9 4.4 %collective-permute-done.17 = f32[27,4,8,128]{3,2,1,0:T(8,128)S(1)} collective-permute-done((f32[27,4,8,128]{3,2,1,0:T(8,128)S(1)}, f32[27,4,8,128]{3,2,1,0:T(8,128)S(1)}, u32[]{:S(2)}, u32[]{:S(2)}) %collective-permute-start.17) | collective-permute-done | bytes 442400 | tf_op jit(solution)/shard_map/two_three_halo/ppermute | solution.py:16
  95.4 6.4 %one_down.1 = (f32[8,128]{1,0:T(8,128)S(1)}, f32[4,16,128]{2,1,0:T(8,128)}) custom-call(s32[2]{0:T(128)S(1)} %pad_add_fusion.pos, f32[14,32,128]{2,1,0:T(8,128)S(1)} %pad_maximum_fusion.9.g.g1, f32[27,12,16,128]{3,2,1,0:T(8,128)} %copy-done.12, f32[27,12,8,128]{3,2,1,0:T(8,128)S(1)} %pad_maximum_fusion.clo, f32[27,12,8,128]{3,2,1,0:T(8,128)S(1)} %pad_maximum_fusion.1.chi), custom_call_target="tpu_custom_call" | custom-call | tf_op jit(solution)/shard_map/one_down/one_down/pallas_call | solution.py:519
  101.8 3.1 %collective-permute-start.19 = (f32[8,128]{1,0:T(8,128)S(1)}, f32[8,128]{1,0:T(8,128)S(1)}, u32[]{:S(2)}, u32[]{:S(2)}) collective-permute-start(f32[8,128]{1,0:T(8,128)S(1)} %get-tuple-element.35), channel_id=1, source_target_pairs={{0,15},{1,0},{2,1},{3,2},{4,3},{5,4},{6,5},{7,6},{8,7},{9,8},{10,9... | collective-permute-start | bytes 12296 | tf_op jit(solution)/shard_map/two_exchange/ppermute | solution.py:16
  104.9 4.1 %collective-permute-start.21 = (f32[2,648,128]{2,1,0:T(8,128)}, f32[2,648,128]{2,1,0:T(8,128)S(1)}, u32[]{:S(2)}, u32[]{:S(2)}) collective-permute-start(f32[2,648,128]{2,1,0:T(8,128)} %get-tuple-element.55), channel_id=1, source_target_pairs={{0,208},{16,224},{32,240},{48,0},{64,16},{80,32},{96,48},{112,64},... | collective-permute-start | bytes 1990664 | tf_op jit(solution)/shard_map/two_halo/ppermute | solution.py:16
  109.1 5.3 %collective-permute-start.23 = (f32[4,16,128]{2,1,0:T(8,128)}, f32[4,16,128]{2,1,0:T(8,128)S(1)}, u32[]{:S(2)}, u32[]{:S(2)}) collective-permute-start(f32[4,16,128]{2,1,0:T(8,128)} %get-tuple-element.38), channel_id=1, source_target_pairs={{0,240},{16,0},{32,16},{48,32},{64,48},{80,64},{96,80},{112,96},{1... | collective-permute-start | bytes 98312 | tf_op jit(solution)/shard_map/one_values/ppermute | solution.py:16
  115.1 3.5 %all-to-all-start = ((f32[16,24,128]{2,1,0:T(8,128)}), f32[16,24,128]{2,1,0:T(8,128)S(1)}, u32[]{:S(2)}, u32[]{:S(2)}) async-start(f32[16,24,128]{2,1,0:T(8,128)} %broadcast_in_dim.4), calls=%async_computation | async-start | bytes 393216 | tf_op jit(solution)/shard_map/two_exchange/all_to_all | solution.py:21
  118.6 5.9 %collective-permute-done.22 = f32[4,16,128]{2,1,0:T(8,128)S(1)} collective-permute-done((f32[4,16,128]{2,1,0:T(8,128)}, f32[4,16,128]{2,1,0:T(8,128)S(1)}, u32[]{:S(2)}, u32[]{:S(2)}) %collective-permute-start.22) | collective-permute-done | bytes 32800 | tf_op jit(solution)/shard_map/one_values/ppermute | solution.py:16
  132.6 3.0 %collective-permute-done.24 = f32[112,128]{1,0:T(8,128)S(1)} collective-permute-done((f32[112,128]{1,0:T(8,128)S(1)}, f32[112,128]{1,0:T(8,128)S(1)}, u32[]{:S(2)}, u32[]{:S(2)}) %collective-permute-start.24) | collective-permute-done | bytes 57376 | tf_op jit(solution)/shard_map/three_exchange/ppermute | solution.py:16
  135.7 3.2 %collective-permute-start.27 = (f32[3,128]{1,0:T(4,128)S(1)}, f32[3,128]{1,0:T(4,128)S(1)}, u32[]{:S(2)}, u32[]{:S(2)}) collective-permute-start(f32[3,128]{1,0:T(4,128)S(1)} %pad_maximum_fusion.20), channel_id=1, source_target_pairs={{0,14},{1,15},{2,0},{3,1},{4,2},{5,3},{6,4},{7,5},{8,6},{9,7},{10,... | collective-permute-start | bytes 4616 | tf_op jit(solution)/shard_map/three_exchange/ppermute | solution.py:16
  141.2 6.7 %all-to-all-start.1 = ((f32[16,32,128]{2,1,0:T(8,128)}), f32[16,32,128]{2,1,0:T(8,128)S(1)}, u32[]{:S(2)}, u32[]{:S(2)}) async-start(f32[16,32,128]{2,1,0:T(8,128)} %broadcast_in_dim.5), calls=%async_computation.1 | async-start | bytes 524288 | tf_op jit(solution)/shard_map/three_exchange/all_to_all | solution.py:21
  148.0 8.7 %all-to-all-done.1.gv = f32[16,32,128]{2,1,0:T(8,128)S(1)} async-done(((f32[16,32,128]{2,1,0:T(8,128)}), f32[16,32,128]{2,1,0:T(8,128)S(1)}, u32[]{:S(2)}, u32[]{:S(2)}) %all-to-all-start.1) | async-done | bytes 262176 | tf_op jit(solution)/shard_map/three_exchange/all_to_all | solution.py:21
  156.6 10.7 %coarse_up.1 = f32[4,16,128]{2,1,0:T(8,128)S(1)} custom-call(s32[2]{0:T(128)S(1)} %pad_add_fusion.pos, f32[16,32,128]{2,1,0:T(8,128)S(1)} %all-to-all-done.1.gv, f32[16,216,128]{2,1,0:T(8,128)} %all-gather.2.cloned.1.call-done.c3, f32[16,24,128]{2,1,0:T(8,128)S(1)} %all-to-all-done.g_all.g2_all, f32[2,648,128]{2,1,0:T(8,128)S(1)} %collective-permute-done.20.far_lo, ...), custom_call_target="tpu_custom_call" | custom-call | tf_op jit(solution)/shard_map/coarse_up/coarse_up/pallas_call | solution.py:519
  171.2 4.6 %collective-permute-done.30 = f32[3,16,128]{2,1,0:T(8,128)S(1)} collective-permute-done((f32[3,16,128]{2,1,0:T(8,128)S(1)}, f32[3,16,128]{2,1,0:T(8,128)S(1)}, u32[]{:S(2)}, u32[]{:S(2)}) %collective-permute-start.30) | collective-permute-done | bytes 24608 | tf_op jit(solution)/shard_map/one_back/ppermute | solution.py:16
  177.5 3.3 %collective-permute-done.32 = f32[10,8,128]{2,1,0:T(8,128)S(1)} collective-permute-done((f32[10,8,128]{2,1,0:T(8,128)S(1)}, f32[10,8,128]{2,1,0:T(8,128)S(1)}, u32[]{:S(2)}, u32[]{:S(2)}) %collective-permute-start.32) | collective-permute-done | bytes 40992 | tf_op jit(solution)/shard_map/one_back/ppermute | solution.py:16
  180.9 5.1 %fine_up.1 = f32[8,32,256]{2,1,0:T(8,128)} custom-call(s32[2]{0:T(128)S(1)} %pad_add_fusion.pos, f32[16,48,256]{2,1,0:T(8,128)S(1)} %copy-done.10, f32[16,48,256]{2,1,0:T(8,128)S(1)} %copy-done.11, f32[16,48,256]{2,1,0:T(8,128)S(1)} %copy-done.8, f32[10,32,128]{2,1,0:T(8,128)S(1)} %pad_maximum_fusion.10.c1), custom_call_target="tpu_custom_call" | custom-call | tf_op jit(solution)/shard_map/fine_up/fine_up/pallas_call | solution.py:519
  (157 shorter events, 30.6 us)
Async XLA Ops:
  6.5 150.1 %all-gather.2.cloned.1.call-start = ((), (), s32[]{:S(2)}) async-start(), calls=%async_computation.2 | async-start | bytes 1880064 | tf_op jit(solution)/shard_map/two_three_halo/all_gather | solution.py:569
  8.0 20.7 %collective-permute-start = (f32[2,7,32,256]{3,2,1,0:T(8,128)S(1)}, f32[2,7,32,256]{3,2,1,0:T(8,128)S(1)}, u32[]{:S(2)}, u32[]{:S(2)}) collective-permute-start(f32[2,7,32,256]{3,2,1,0:T(8,128)S(1)} %pad_maximum_fusion.4), channel_id=1, source_target_pairs={{0,16},{16,32},{32,48},{48,64},{64,80},{80,96},{96,112},{112,128},... | collective-permute-start | bytes 1376264 | tf_op jit(solution)/shard_map/fine_halo/ppermute | solution.py:16
  8.9 19.7 %collective-permute-start.1 = (f32[2,7,32,256]{3,2,1,0:T(8,128)}, f32[2,7,32,256]{3,2,1,0:T(8,128)S(1)}, u32[]{:S(2)}, u32[]{:S(2)}) collective-permute-start(f32[2,7,32,256]{3,2,1,0:T(8,128)} %pad_maximum_fusion.5), channel_id=1, source_target_pairs={{0,240},{16,0},{32,16},{48,32},{64,48},{80,64},{96,80},{112,96},{1... | collective-permute-start | bytes 1376264 | tf_op jit(solution)/shard_map/fine_halo/ppermute | solution.py:16
  14.5 5.7 %collective-permute-start.11 = (f32[248,128]{1,0:T(8,128)S(1)}, f32[248,128]{1,0:T(8,128)S(1)}, u32[]{:S(2)}, u32[]{:S(2)}) collective-permute-start(f32[248,128]{1,0:T(8,128)S(1)} %pad_maximum_fusion.11), channel_id=1, source_target_pairs={{0,15},{1,0},{2,1},{3,2},{4,3},{5,4},{6,5},{7,6},{8,7},{9,8},{10,9... | collective-permute-start | bytes 380936 | tf_op jit(solution)/shard_map/two_three_halo/ppermute | solution.py:16
  17.7 5.6 %collective-permute-start.10 = (f32[248,128]{1,0:T(8,128)S(1)}, f32[248,128]{1,0:T(8,128)S(1)}, u32[]{:S(2)}, u32[]{:S(2)}) collective-permute-start(f32[248,128]{1,0:T(8,128)S(1)} %pad_maximum_fusion.11), channel_id=1, source_target_pairs={{0,1},{1,2},{2,3},{3,4},{4,5},{5,6},{6,7},{7,8},{8,9},{9,10},{10,1... | collective-permute-start | bytes 380936 | tf_op jit(solution)/shard_map/two_three_halo/ppermute | solution.py:16
  23.3 5.4 %collective-permute-start.28 = (f32[3,32,128]{2,1,0:T(8,128)S(1)}, f32[3,32,128]{2,1,0:T(8,128)S(1)}, u32[]{:S(2)}, u32[]{:S(2)}) collective-permute-start(f32[3,32,128]{2,1,0:T(8,128)S(1)} %pad_maximum_fusion.16), channel_id=1, source_target_pairs={{0,2},{1,3},{2,4},{3,5},{4,6},{5,7},{6,8},{7,9},{8,10},{9,11},{10,... | collective-permute-start | bytes 147464 | tf_op jit(solution)/shard_map/two_three_halo/ppermute | solution.py:16
  23.4 12.2 %collective-permute-start.29 = (f32[3,32,128]{2,1,0:T(8,128)S(1)}, f32[3,32,128]{2,1,0:T(8,128)S(1)}, u32[]{:S(2)}, u32[]{:S(2)}) collective-permute-start(f32[3,32,128]{2,1,0:T(8,128)S(1)} %pad_maximum_fusion.16), channel_id=1, source_target_pairs={{0,14},{1,15},{2,0},{3,1},{4,2},{5,3},{6,4},{7,5},{8,6},{9,7},{10,... | collective-permute-start | bytes 147464 | tf_op jit(solution)/shard_map/two_three_halo/ppermute | solution.py:16
  30.3 22.1 %collective-permute-start.4 = (f32[27,4,16,128]{3,2,1,0:T(8,128)S(1)}, f32[27,4,16,128]{3,2,1,0:T(8,128)}, u32[]{:S(2)}, u32[]{:S(2)}) collective-permute-start(f32[27,4,16,128]{3,2,1,0:T(8,128)S(1)} %copy-done.13), channel_id=1, source_target_pairs={{0,16},{16,32},{32,48},{48,64},{64,80},{80,96},{96,112},{112,128},... | collective-permute-start | bytes 2654216 | tf_op jit(solution)/shard_map/one_halo/ppermute | solution.py:16
  30.3 22.1 %collective-permute-start.5 = (f32[27,4,16,128]{3,2,1,0:T(8,128)S(1)}, f32[27,4,16,128]{3,2,1,0:T(8,128)}, u32[]{:S(2)}, u32[]{:S(2)}) collective-permute-start(f32[27,4,16,128]{3,2,1,0:T(8,128)S(1)} %copy-done.13), channel_id=1, source_target_pairs={{0,240},{16,0},{32,16},{48,32},{64,48},{80,64},{96,80},{112,96},{1... | collective-permute-start | bytes 2654216 | tf_op jit(solution)/shard_map/one_halo/ppermute | solution.py:16
  35.6 8.3 %collective-permute-start.2 = (f32[2,22,8,256]{3,2,1,0:T(8,128)}, f32[2,22,8,256]{3,2,1,0:T(8,128)S(1)}, u32[]{:S(2)}, u32[]{:S(2)}) collective-permute-start(f32[2,22,8,256]{3,2,1,0:T(8,128)} %pad_maximum_fusion.6), channel_id=1, source_target_pairs={{0,1},{1,2},{2,3},{3,4},{4,5},{5,6},{6,7},{7,8},{8,9},{9,10},{10,1... | collective-permute-start | bytes 1081352 | tf_op jit(solution)/shard_map/fine_halo/ppermute | solution.py:16
  35.7 8.3 %collective-permute-start.3 = (f32[2,22,8,256]{3,2,1,0:T(8,128)}, f32[2,22,8,256]{3,2,1,0:T(8,128)S(1)}, u32[]{:S(2)}, u32[]{:S(2)}) collective-permute-start(f32[2,22,8,256]{3,2,1,0:T(8,128)} %pad_maximum_fusion.7), channel_id=1, source_target_pairs={{0,15},{1,0},{2,1},{3,2},{4,3},{5,4},{6,5},{7,6},{8,7},{9,8},{10,9... | collective-permute-start | bytes 1081352 | tf_op jit(solution)/shard_map/fine_halo/ppermute | solution.py:16
  54.5 8.3 %collective-permute-start.7 = (f32[5,16,128]{2,1,0:T(8,128)S(1)}, f32[5,16,128]{2,1,0:T(8,128)S(1)}, u32[]{:S(2)}, u32[]{:S(2)}) collective-permute-start(f32[5,16,128]{2,1,0:T(8,128)S(1)} %get-tuple-element.82), channel_id=1, source_target_pairs={{0,240},{16,0},{32,16},{48,32},{64,48},{80,64},{96,80},{112,96},{1... | collective-permute-start | bytes 122888 | tf_op jit(solution)/shard_map/one_exchange/ppermute | solution.py:16
  59.9 7.3 %collective-permute-start.6 = (f32[5,16,128]{2,1,0:T(8,128)S(1)}, f32[5,16,128]{2,1,0:T(8,128)S(1)}, u32[]{:S(2)}, u32[]{:S(2)}) collective-permute-start(f32[5,16,128]{2,1,0:T(8,128)S(1)} %get-tuple-element.81), channel_id=1, source_target_pairs={{0,16},{16,32},{32,48},{48,64},{64,80},{80,96},{96,112},{112,128},... | collective-permute-start | bytes 122888 | tf_op jit(solution)/shard_map/one_exchange/ppermute | solution.py:16
  62.9 27.8 %collective-permute-start.14 = (f32[27,8,8,128]{3,2,1,0:T(8,128)S(1)}, f32[27,8,8,128]{3,2,1,0:T(8,128)S(1)}, u32[]{:S(2)}, u32[]{:S(2)}) collective-permute-start(f32[27,8,8,128]{3,2,1,0:T(8,128)S(1)} %get-tuple-element.40), channel_id=1, source_target_pairs={{0,1},{1,2},{2,3},{3,4},{4,5},{5,6},{6,7},{7,8},{8,9},{9,10},{10,1... | collective-permute-start | bytes 2654216 | tf_op jit(solution)/shard_map/one_halo/ppermute | solution.py:16
  67.3 7.6 %collective-permute-start.9 = (f32[14,8,128]{2,1,0:T(8,128)S(1)}, f32[14,8,128]{2,1,0:T(8,128)S(1)}, u32[]{:S(2)}, u32[]{:S(2)}) collective-permute-start(f32[14,8,128]{2,1,0:T(8,128)S(1)} %get-tuple-element.68), channel_id=1, source_target_pairs={{0,15},{1,0},{2,1},{3,2},{4,3},{5,4},{6,5},{7,6},{8,7},{9,8},{10,9... | collective-permute-start | bytes 172040 | tf_op jit(solution)/shard_map/one_exchange/ppermute | solution.py:16
  67.4 20.2 %collective-permute-start.13 = (f32[648,128]{1,0:T(8,128)S(1)}, f32[648,128]{1,0:T(8,128)S(1)}, u32[]{:S(2)}, u32[]{:S(2)}) collective-permute-start(f32[648,128]{1,0:T(8,128)S(1)} %pad_maximum_fusion.8.own), channel_id=1, source_target_pairs={{0,16},{16,32},{32,48},{48,64},{64,80},{80,96},{96,112},{112,128},... | collective-permute-start | bytes 995336 | tf_op jit(solution)/shard_map/two_halo/ppermute | solution.py:16
  67.5 21.9 %collective-permute-start.12 = (f32[648,128]{1,0:T(8,128)S(1)}, f32[648,128]{1,0:T(8,128)S(1)}, u32[]{:S(2)}, u32[]{:S(2)}) collective-permute-start(f32[648,128]{1,0:T(8,128)S(1)} %pad_maximum_fusion.8.own), channel_id=1, source_target_pairs={{0,240},{16,0},{32,16},{48,32},{64,48},{80,64},{96,80},{112,96},{1... | collective-permute-start | bytes 995336 | tf_op jit(solution)/shard_map/two_halo/ppermute | solution.py:16
  72.8 18.0 %collective-permute-start.16 = (f32[27,8,8,128]{3,2,1,0:T(8,128)S(1)}, f32[27,8,8,128]{3,2,1,0:T(8,128)S(1)}, u32[]{:S(2)}, u32[]{:S(2)}) collective-permute-start(f32[27,8,8,128]{3,2,1,0:T(8,128)S(1)} %get-tuple-element.39), channel_id=1, source_target_pairs={{0,15},{1,0},{2,1},{3,2},{4,3},{5,4},{6,5},{7,6},{8,7},{9,8},{10,9... | collective-permute-start | bytes 2654216 | tf_op jit(solution)/shard_map/one_halo/ppermute | solution.py:16
  74.8 4.8 %collective-permute-start.8 = (f32[14,8,128]{2,1,0:T(8,128)S(1)}, f32[14,8,128]{2,1,0:T(8,128)S(1)}, u32[]{:S(2)}, u32[]{:S(2)}) collective-permute-start(f32[14,8,128]{2,1,0:T(8,128)S(1)} %get-tuple-element.67), channel_id=1, source_target_pairs={{0,1},{1,2},{2,3},{3,4},{4,5},{5,6},{6,7},{7,8},{8,9},{9,10},{10,1... | collective-permute-start | bytes 172040 | tf_op jit(solution)/shard_map/one_exchange/ppermute | solution.py:16
  79.6 11.1 %collective-permute-start.15 = (f32[27,4,8,128]{3,2,1,0:T(8,128)S(1)}, f32[27,4,8,128]{3,2,1,0:T(8,128)S(1)}, u32[]{:S(2)}, u32[]{:S(2)}) collective-permute-start(f32[27,4,8,128]{3,2,1,0:T(8,128)S(1)} %get-tuple-element.44), channel_id=1, source_target_pairs={{0,1},{1,2},{2,3},{3,4},{4,5},{5,6},{6,7},{7,8},{8,9},{9,10},{10,1... | collective-permute-start | bytes 1327112 | tf_op jit(solution)/shard_map/two_three_halo/ppermute | solution.py:16
  87.6 7.7 %collective-permute-start.17 = (f32[27,4,8,128]{3,2,1,0:T(8,128)S(1)}, f32[27,4,8,128]{3,2,1,0:T(8,128)S(1)}, u32[]{:S(2)}, u32[]{:S(2)}) collective-permute-start(f32[27,4,8,128]{3,2,1,0:T(8,128)S(1)} %get-tuple-element.43), channel_id=1, source_target_pairs={{0,15},{1,0},{2,1},{3,2},{4,3},{5,4},{6,5},{7,6},{8,7},{9,8},{10,9... | collective-permute-start | bytes 1327112 | tf_op jit(solution)/shard_map/two_three_halo/ppermute | solution.py:16
  101.8 7.3 %collective-permute-start.19 = (f32[8,128]{1,0:T(8,128)S(1)}, f32[8,128]{1,0:T(8,128)S(1)}, u32[]{:S(2)}, u32[]{:S(2)}) collective-permute-start(f32[8,128]{1,0:T(8,128)S(1)} %get-tuple-element.35), channel_id=1, source_target_pairs={{0,15},{1,0},{2,1},{3,2},{4,3},{5,4},{6,5},{7,6},{8,7},{9,8},{10,9... | collective-permute-start | bytes 12296 | tf_op jit(solution)/shard_map/two_exchange/ppermute | solution.py:16
  104.9 9.5 %collective-permute-start.18 = (f32[8,128]{1,0:T(8,128)S(1)}, f32[8,128]{1,0:T(8,128)S(1)}, u32[]{:S(2)}, u32[]{:S(2)}) collective-permute-start(f32[8,128]{1,0:T(8,128)S(1)} %get-tuple-element.35), channel_id=1, source_target_pairs={{0,1},{1,2},{2,3},{3,4},{4,5},{5,6},{6,7},{7,8},{8,9},{9,10},{10,1... | collective-permute-start | bytes 12296 | tf_op jit(solution)/shard_map/two_exchange/ppermute | solution.py:16
  104.9 20.4 %collective-permute-start.20 = (f32[2,648,128]{2,1,0:T(8,128)}, f32[2,648,128]{2,1,0:T(8,128)S(1)}, u32[]{:S(2)}, u32[]{:S(2)}) collective-permute-start(f32[2,648,128]{2,1,0:T(8,128)} %get-tuple-element.56), channel_id=1, source_target_pairs={{0,48},{16,64},{32,80},{48,96},{64,112},{80,128},{96,144},{112,160... | collective-permute-start | bytes 1990664 | tf_op jit(solution)/shard_map/two_halo/ppermute | solution.py:16
  104.9 20.4 %collective-permute-start.21 = (f32[2,648,128]{2,1,0:T(8,128)}, f32[2,648,128]{2,1,0:T(8,128)S(1)}, u32[]{:S(2)}, u32[]{:S(2)}) collective-permute-start(f32[2,648,128]{2,1,0:T(8,128)} %get-tuple-element.55), channel_id=1, source_target_pairs={{0,208},{16,224},{32,240},{48,0},{64,16},{80,32},{96,48},{112,64},... | collective-permute-start | bytes 1990664 | tf_op jit(solution)/shard_map/two_halo/ppermute | solution.py:16
  109.1 15.4 %collective-permute-start.22 = (f32[4,16,128]{2,1,0:T(8,128)}, f32[4,16,128]{2,1,0:T(8,128)S(1)}, u32[]{:S(2)}, u32[]{:S(2)}) collective-permute-start(f32[4,16,128]{2,1,0:T(8,128)} %get-tuple-element.38), channel_id=1, source_target_pairs={{0,16},{16,32},{32,48},{48,64},{64,80},{80,96},{96,112},{112,128},... | collective-permute-start | bytes 98312 | tf_op jit(solution)/shard_map/one_values/ppermute | solution.py:16
  109.1 16.2 %collective-permute-start.23 = (f32[4,16,128]{2,1,0:T(8,128)}, f32[4,16,128]{2,1,0:T(8,128)S(1)}, u32[]{:S(2)}, u32[]{:S(2)}) collective-permute-start(f32[4,16,128]{2,1,0:T(8,128)} %get-tuple-element.38), channel_id=1, source_target_pairs={{0,240},{16,0},{32,16},{48,32},{64,48},{80,64},{96,80},{112,96},{1... | collective-permute-start | bytes 98312 | tf_op jit(solution)/shard_map/one_values/ppermute | solution.py:16
  115.1 11.8 %all-to-all-start = ((f32[16,24,128]{2,1,0:T(8,128)}), f32[16,24,128]{2,1,0:T(8,128)S(1)}, u32[]{:S(2)}, u32[]{:S(2)}) async-start(f32[16,24,128]{2,1,0:T(8,128)} %broadcast_in_dim.4), calls=%async_computation | async-start | bytes 393216 | tf_op jit(solution)/shard_map/two_exchange/all_to_all | solution.py:21
  135.6 4.9 %collective-permute-start.26 = (f32[3,128]{1,0:T(4,128)S(1)}, f32[3,128]{1,0:T(4,128)S(1)}, u32[]{:S(2)}, u32[]{:S(2)}) collective-permute-start(f32[3,128]{1,0:T(4,128)S(1)} %pad_maximum_fusion.20), channel_id=1, source_target_pairs={{0,2},{1,3},{2,4},{3,5},{4,6},{5,7},{6,8},{7,9},{8,10},{9,11},{10,... | collective-permute-start | bytes 4616 | tf_op jit(solution)/shard_map/three_exchange/ppermute | solution.py:16
  141.2 15.4 %all-to-all-start.1 = ((f32[16,32,128]{2,1,0:T(8,128)}), f32[16,32,128]{2,1,0:T(8,128)S(1)}, u32[]{:S(2)}, u32[]{:S(2)}) async-start(f32[16,32,128]{2,1,0:T(8,128)} %broadcast_in_dim.5), calls=%async_computation.1 | async-start | bytes 524288 | tf_op jit(solution)/shard_map/three_exchange/all_to_all | solution.py:21
  168.7 7.1 %collective-permute-start.30 = (f32[3,16,128]{2,1,0:T(8,128)S(1)}, f32[3,16,128]{2,1,0:T(8,128)S(1)}, u32[]{:S(2)}, u32[]{:S(2)}) collective-permute-start(f32[3,16,128]{2,1,0:T(8,128)S(1)} %get-tuple-element.79), channel_id=1, source_target_pairs={{0,16},{16,32},{32,48},{48,64},{64,80},{80,96},{96,112},{112,128},... | collective-permute-start | bytes 73736 | tf_op jit(solution)/shard_map/one_back/ppermute | solution.py:16
  175.9 5.0 %collective-permute-start.32 = (f32[10,8,128]{2,1,0:T(8,128)S(1)}, f32[10,8,128]{2,1,0:T(8,128)S(1)}, u32[]{:S(2)}, u32[]{:S(2)}) collective-permute-start(f32[10,8,128]{2,1,0:T(8,128)S(1)} %get-tuple-element.71), channel_id=1, source_target_pairs={{0,1},{1,2},{2,3},{3,4},{4,5},{5,6},{6,7},{7,8},{8,9},{9,10},{10,1... | collective-permute-start | bytes 122888 | tf_op jit(solution)/shard_map/one_back/ppermute | solution.py:16
  (27 other events, 246.8 us)
Sparse Core Ops, SparseCore 0:
  39.5 47.3 all-gather.1

commit v2 on v1

--- a/solution.py
+++ b/solution.py
@@ -276,19 +276,7 @@
 
 
 def two_coefficient(c2, block, k):
-    ref, index = c2[block]
-    parts = []
-    for j in range(3):
-        rows = pl.ds((j * 27 + k) * 8, 8)
-        parts.append(ref[rows, :] if index is None else ref[index, rows, :])
-    return jnp.concatenate(parts, axis=0)
-
-
-def two_blocks(far_lo, before, own, after, far_hi):
-    return [(far_lo, 0), (far_lo, 1), (before, None), (own, None), (after, None)] + [
-        (far_hi, 0),
-        (far_hi, 1),
-    ]
+    return jnp.concatenate([ref[block, pl.ds(k * 8, 8), :] for ref in c2], axis=0)
 
 
 def two_weights(w, c2, ix, iy):
@@ -346,14 +334,14 @@
 
 
 def two_sources(g, own, ix):
-    batch(0, 7, 7, lambda b: g[jnp.clip(ix + b - 3, 0, 15)], put(own))
+    batch(0, 7, 7, lambda b: g[jnp.clip(ix + b - 3, 0, 15), 0:24], put(own))
 
 
 def two_down(
-    pos, g_all, far_lo, before, own, after, far_hi, g_out, v_out, v, vx, w, g, t
+    pos, g_all, c2lo, c2own, c2hi, g_out, v_out, v, vx, w, g, t
 ):
     ix, iy = pos[0], pos[1]
-    c2 = two_blocks(far_lo, before, own, after, far_hi)
+    c2 = (c2lo, c2own, c2hi)
     two_weights(w, c2, ix, iy)
     two_sources(g_all, g, ix)
     for b in (0, 8):
@@ -378,89 +366,83 @@
     g_out[...] = jnp.broadcast_to(jnp.sum(y, axis=0, keepdims=True), (8, 128))
 
 
-def three_y(c):
-    lane = iota(c.shape, 1)
-    rows = c.shape[0]
-    down = pltpu.roll(c, 32, 1)
-    below = jnp.where(lane >= 32, down, pltpu.roll(down, 1, 0))
-    up = pltpu.roll(c, 96, 1)
-    above = jnp.where(lane < 96, up, pltpu.roll(up, rows - 1, 0))
+def three_y(v, b):
+    lane = iota((16, 128), 1)
+    below = jnp.where(lane >= 32, pltpu.roll(v[b], 32, 1), pltpu.roll(v[b - 1], 32, 1))
+    above = jnp.where(lane < 96, pltpu.roll(v[b], 96, 1), pltpu.roll(v[b + 1], 96, 1))
     return below, above
 
 
+def three_x(c):
+    row = iota((16, 128), 0)
+    before = jnp.where(row > 0, pltpu.roll(c, 1, 0), 0.0)
+    after = jnp.where(row < 15, pltpu.roll(c, 15, 0), 0.0)
+    return before, after
+
+
 def three_solve(v, vx, w, g, c3, iy):
-    yb = iota((8, 128), 0)
-    ok = (yb + iy >= 3) & (yb + iy < 19) & (yb < 7)
-
-    def coefficient(x, k):
-        return c3[x, pl.ds(k * 8, 8), :]
-
-    for x in (0, 17):
-        v[x] = jnp.zeros((8, 128), F32)
-        for k in range(9):
-            vx[k, x] = jnp.zeros((8, 128), F32)
-    batch(
-        0, 16, 16, lambda x: jnp.where(ok, RELAXATION / coefficient(x, 13), 0.0), put(w)
-    )
-    for x in range(16):
-        v[x + 1] = w[x] * g[x, 0:8]
-
-    def spread(x):
-        c = v[x]
-        below, above = three_y(c)
+    def coefficient(b, k):
+        ref, index = c3[b]
+        return ref[index, k]
+
+    for b in (0, 8):
+        v[b] = jnp.zeros((16, 128), F32)
+    for b in range(7):
+        ok = between(iy + b - 3, 16)
+        w[b] = jnp.where(ok, RELAXATION / coefficient(b, 13), 0.0)
+        v[b + 1] = w[b] * g[b]
+
+    def spread(b):
+        below, above = three_y(v, b)
         values = []
-        for plane in (below, c, above):
+        for plane in (below, v[b], above):
             left, right = z_shifts(plane, 32)
             values += [left, plane, right]
         return values
 
-    def keep(x, values):
+    def keep(b, values):
         for k in range(9):
-            vx[k, x] = values[k]
-
-    def update(x):
+            vx[k, b - 1] = values[k]
+
+    def update(b):
         parts = []
-        for a in range(3):
-            part = None
-            for m in range(9):
-                k = 9 * a + m
-                if k == 13:
-                    continue
-                term = coefficient(x - 1, k) * vx[m, x + a - 1]
-                part = term if part is None else part + term
+        for m in range(9):
+            plane = vx[m, b - 1]
+            before, after = three_x(plane)
+            part = coefficient(b - 1, m) * before + coefficient(b - 1, 18 + m) * after
+            if m != 4:
+                part = part + coefficient(b - 1, 9 + m) * plane
             parts.append(part)
-        rest = parts[0] + parts[1] + parts[2]
-        return KEEP * v[x] + w[x - 1] * (g[x - 1, 0:8] - rest)
+        rest = parts[0]
+        for part in parts[1:]:
+            rest = rest + part
+        return KEEP * v[b] + w[b - 1] * (g[b - 1] - rest)
 
     def sweep(_, carry):
-        for x in (1, 5, 9, 13):
-            batch(x, x + 4, 4, spread, keep)
-        for x in (1, 5, 9, 13):
-            batch(x, x + 4, 4, update, put(v))
+        batch(1, 8, 7, spread, keep)
+        batch(1, 8, 7, update, put(v))
         return carry
 
     lax.fori_loop(0, 7, sweep, 0)
 
 
 def coarse_up(
-    pos, gv, c3, g2_all, far_lo, before, own, after, far_hi, g1, v1, v1lo, v1hi,
+    pos, g3, v2, c3lo, c3own, c3hi, g2_all, c2lo, c2own, c2hi, g1, v1, v1lo, v1hi,
     cx, clo, chi, out,
-    s3, vx3, w3, e, d, pc, s2, vx2, w2, g2, u, s1, vz, w1,
+    s3, vx3, w3, e, pc, s2, vx2, w2, g2, u, s1, vz, w1,
 ):
     ix, iy = pos[0], pos[1]
-    c2 = two_blocks(far_lo, before, own, after, far_hi)
-    three_solve(s3, vx3, w3, gv, c3, iy)
+    c2 = (c2lo, c2own, c2hi)
+    c3 = [(c3lo, 0), (c3lo, 1), (c3own, 0), (c3own, 1), (c3own, 2), (c3hi, 0), (c3hi, 1)]
+    three_solve(s3, vx3, w3, g3, c3, iy)
     two_weights(w2, c2, ix, iy)
     two_sources(g2_all, g2, ix)
     one_weights(w1, cx, clo, chi, ix, iy)
-    for j in range(9):
-        x = jnp.clip(ix + j - 4, 0, 15)
-        mid = 0.75 * s3[x + 1]
-        for p in range(2):
-            c = mid + 0.25 * s3[x + 2 * p]
-            below, above = three_y(c)
-            e[0, j, :, p * 128 : p * 128 + 128] = 0.75 * c + 0.25 * below
-            e[1, j, :, p * 128 : p * 128 + 128] = 0.75 * c + 0.25 * above
+    for b in range(3):
+        for s, moved in enumerate(three_y(s3, b + 3)):
+            c = 0.75 * s3[b + 3] + 0.25 * moved
+            for p, beside in enumerate(three_x(c)):
+                e[s, b, :, p * 128 : p * 128 + 128] = 0.75 * c + 0.25 * beside
     for q in range(4):
 
         def entry(r, m):
@@ -469,16 +451,16 @@
 
         pz2 = matrix(256, 128, entry)
         for s in range(2):
-            d[4 * s + q] = dot(e[s].reshape(72, 256), pz2).reshape(9, 8, 128)
-    for s in range(2):
-        for q in range(4):
-            for j in range(9):
-                pc[j, pl.ds(2 * q + s, 8, stride=8), :] = d[4 * s + q, j]
+            grown = dot(e[s].reshape(48, 256), pz2)
+            for b in range(3):
+                rows = pl.ds(8 * b + 2 * q + s, 16, stride=24)
+                pc[rows, :] = grown[16 * b : 16 * b + 16]
     row_two = rows_valid((24, 128), iy * 8 - 8, 128)
     for j in range(9):
         ok = row_two & between(ix + j - 4, 16)
-        held = gv[jnp.clip(ix + j - 4, 0, 15), 8:32]
-        s2[j] = jnp.where(ok, held + pc[j, 16:40], 0.0)
+        x = jnp.clip(ix + j - 4, 0, 15)
+        rows = pl.ds(pl.multiple_of(x * 24, 8), 24)
+        s2[j] = jnp.where(ok, v2[x] + pc[rows, :], 0.0)
     for lo, hi in ((1, 8), (2, 7)):
         twice(lambda: two_sweep(s2, vx2, w2, g2, c2, lo, hi))
     low = iota((24, 128), 1) < 64
@@ -556,18 +538,10 @@
         coarse_two, coarse_three, one = lax.optimization_barrier(
             (coarse_two, coarse_three, coarse_one, last, first)
         )[:3]
-        c2 = jnp.concatenate([coarse_two[:, 0], coarse_two[:, 1]], axis=-1)
+        c2 = jnp.concatenate([coarse_two[:, 0], coarse_two[:, 1]], axis=-1).reshape(216, 128)
         c3 = jnp.concatenate([coarse_three[:, 0, i] for i in range(4)], axis=-1)
-        c3 = jnp.pad(c3, ((0, 5), (0, 0)))
-        own = jnp.concatenate([c2.reshape(216, 128), c3], axis=0)
-        before, after = ring(own, "gy", 1), ring(own, "gy", -1)
-        two = jnp.concatenate([before[:216], own[:216], after[:216]])
-        three = jnp.stack([before[216:], c3, after[216:]])
-        far_before, far_after = ring(three, "gy", 2), ring(three, "gy", -2)
-        seven = jnp.concatenate([far_before[:2], three, far_after[1:], c3[None]])
-        seven = jnp.transpose(seven[:, :27], (1, 0, 2)).reshape(216, 128)
-        c3 = lax.all_gather(seven, "gx")
-        one_lo, one_hi = both(one, "gy", 2, 8)
+        load = jnp.concatenate([one.reshape(1728, 128), c2])
+        xb, xa = ring(load, "gx", 1), ring(load, "gx", -1)
 
     with jax.named_scope("fine_halo"):
         edge = []
@@ -575,9 +549,7 @@
             mid = jnp.stack([source[:, rows], damping[:, rows]])
             edge.append(jnp.concatenate([xlo[:, :, rows], mid, xhi[:, :, rows]], axis=1))
         ylo, yhi = ring(edge[0], "gy", 1), ring(edge[1], "gy", -1)
-
-    with jax.named_scope("one_halo"):
-        cxlo, cxhi = both(after_all(coarse_one, *edge), "gx", 1, 4)
+        yb, ya = both(after_all(coarse_one, *edge), "gy", 2, 8)
 
     with jax.named_scope("fine_down"):
         v0, g1, s0, w0 = call(
@@ -588,28 +560,42 @@
         )
 
     with jax.named_scope("one_halo"):
-        cxlo, cxhi, g1 = lax.optimization_barrier((cxlo, cxhi, g1))
-        sides = jnp.concatenate([cxlo, cxhi], axis=1)
-        side_lo, side_hi = both(sides, "gy", 2, 8)
-        cx = jnp.concatenate([cxlo, coarse_one, cxhi], axis=1)
+        xb, xa, yb, ya, g1 = lax.optimization_barrier((xb, xa, yb, ya, g1))
 
     with jax.named_scope("one_exchange"):
-        edge_lo = RELAXATION * g1[0:1] / cxlo[13, 3:4]
-        edge_hi = RELAXATION * g1[5:6] / cxhi[13, 0:1]
+        at = 13 * 64
+        edge_lo = RELAXATION * g1[0:1] / xb[at + 48 : at + 64].reshape(1, 16, 128)
+        edge_hi = RELAXATION * g1[5:6] / xa[at : at + 16].reshape(1, 16, 128)
         up = jnp.concatenate([edge_lo, g1[1:5]])
         down = jnp.concatenate([g1[1:5], edge_hi])
         before, after = ring(up, "gx", 1), ring(down, "gx", -1)
-        g1e = wide(jnp.concatenate([before, g1[1:5], after]), "gy", 1, 8)
+        xb, xa = lax.optimization_barrier((xb, xa, up, down))[:2]
+        cxlo, cxhi = xb[:1728].reshape(27, 4, 16, 128), xa[:1728].reshape(27, 4, 16, 128)
+        tlo, thi = xb[1728:], xa[1728:]
+        one_lo, one_hi = yb, ya
+        sides = jnp.concatenate([cxlo, cxhi], axis=1)
+        g1x = jnp.concatenate([before, g1[1:5], after])
+        rows = [slice(8, 16), slice(0, 8)]
+        up, down = [
+            jnp.concatenate([sides[:, :, r].reshape(1728, 128), g1x[:, r].reshape(112, 128)])
+            for r in rows
+        ]
+        up, down = ring(up, "gy", 1), ring(down, "gy", -1)
+        g1e = jnp.concatenate(
+            [up[1728:].reshape(14, 8, 128), g1x, down[1728:].reshape(14, 8, 128)], axis=1
+        )
+        side_lo, side_hi = [p[:1728].reshape(27, 8, 8, 128) for p in (up, down)]
 
     with jax.named_scope("two_halo"):
-        two = after_all(two, up, down)
-        tlo, thi = ring(two, "gx", 1), ring(two, "gx", -1)
-        above, below = jnp.stack([two, thi]), jnp.stack([tlo, two])
-        far_lo, far_hi = ring(above, "gx", 3), ring(below, "gx", -3)
-        blocks = (far_lo, tlo, two, thi, far_hi)
+        tlo, thi = lax.optimization_barrier((tlo, thi, before, after))[:2]
+        far_lo = ring(jnp.stack([c2, thi]), "gx", 3)
+        far_hi = ring(jnp.stack([tlo, c2]), "gx", -3)
+        far_lo, far_hi = lax.optimization_barrier((far_lo, far_hi, g1e))[:2]
+        c2own = jnp.concatenate([far_lo, tlo[None], c2[None], thi[None], far_hi])
+        c2lo, c2hi = ring(c2own, "gy", 1), ring(c2own, "gy", -1)
 
     with jax.named_scope("one_down"):
-        g1e = after_all(g1e, above, below)
+        cx = jnp.concatenate([after_all(cxlo, before), coarse_one, cxhi], axis=1)
         clo = jnp.concatenate([side_lo[:, :4], one_lo, side_lo[:, 4:]], axis=1)
         chi = jnp.concatenate([side_hi[:, :4], one_hi, side_hi[:, 4:]], axis=1)
         g2, v1 = call(
@@ -619,10 +605,16 @@
         )
 
     with jax.named_scope("two_exchange"):
-        g2e = everyone(wide(g2, "gy", 0, 8), "gx")
+        load = jnp.concatenate([wide(g2, "gy", 0, 8), jnp.pad(c3, ((0, 5), (0, 0)))])
+        load, c2lo, c2hi = lax.optimization_barrier((load, c2lo, c2hi))
+        g2e = everyone(load, "gx")
+
+    with jax.named_scope("three_halo"):
+        c3x = jnp.transpose(g2e[:, 24:51], (1, 0, 2)).reshape(432, 128)
+        three_lo, three_hi = ring(c3x, "gy", 1), ring(c3x, "gy", -1)
 
     with jax.named_scope("one_values"):
-        v1 = wide(v1, "gx", 0, 4)
+        v1b, v1a = both(v1, "gx", 0, 4)
 
     with jax.named_scope("two_down"):
         g3, v2 = call(
@@ -631,33 +623,44 @@
                 vm(9, 24, 128), vm(9, 9, 24, 128), vm(7, 24, 128), vm(7, 24, 128),
                 vm(1, 24, 128),
             ],
-            pos, g2e, *blocks,
+            pos, g2e, c2lo, c2own, c2hi,
         )
 
     with jax.named_scope("three_exchange"):
+        v1b, v1a = lax.optimization_barrier((v1b, v1a, g3))[:2]
+        v1 = jnp.concatenate([v1b, v1, v1a])
         up = jnp.concatenate([g3, v2, v1[:, 8:].reshape(96, 128)])
         down = jnp.concatenate([g3, v2, v1[:, :8].reshape(96, 128)])
         before, after = ring(up, "gy", 1), ring(down, "gy", -1)
         v1lo, v1hi = before[16:].reshape(12, 8, 128), after[16:].reshape(12, 8, 128)
+        three_lo, three_hi, before, after = lax.optimization_barrier(
+            (three_lo, three_hi, before, after)
+        )
+        c3own = jnp.stack([three_lo, c3x, three_hi]).reshape(3, 27, 16, 128)
         trip = jnp.concatenate([before[:1], g3[:1], after[:1]])
         far_before, far_after = ring(trip, "gy", 2), ring(trip, "gy", -2)
+        c3up, c3down = c3own[:2].reshape(864, 128), c3own[1:].reshape(864, 128)
+        g3, c3up, c3down = lax.optimization_barrier((g3, c3up, c3down))
+        c3lo = ring(c3up, "gy", 2).reshape(2, 27, 16, 128)
+        c3hi = ring(c3down, "gy", -2).reshape(2, 27, 16, 128)
         gv = everyone(
             jnp.concatenate(
                 [far_before[:2], trip, far_after[1:], g3[:1], before[8:16], v2, after[8:16]]
             ),
             "gx",
         )
+        g3e, v2e = jnp.transpose(gv[:, :7], (1, 0, 2)), gv[:, 8:]
 
     with jax.named_scope("coarse_up"):
         (c1,) = call(
             coarse_up, "coarse_up", [(4, 16, 128)],
             [
-                vm(18, 8, 128), vm(9, 18, 8, 128), vm(16, 8, 128), vm(2, 9, 8, 256),
-                vm(8, 9, 8, 128), vm(9, 64, 128),
+                vm(9, 16, 128), vm(9, 7, 16, 128), vm(7, 16, 128), vm(2, 3, 16, 256),
+                vm(384, 128),
                 vm(9, 24, 128), vm(9, 9, 24, 128), vm(7, 24, 128), vm(7, 24, 128),
                 vm(12, 32, 128), vm(12, 32, 128), vm(3, 12, 32, 128), vm(12, 32, 128),
             ],
-            pos, gv, c3, g2e, *blocks, g1e, v1, v1lo, v1hi, cx, clo, chi,
+            pos, g3e, v2e, c3lo, c3own, c3hi, g2e, c2lo, c2own, c2hi, g1e, v1, v1lo, v1hi, cx, clo, chi,
         )
 
     with jax.named_scope("one_back"):

time: 193 us -> 165 us (0.85)
  the two profiles are of different devices: /device:TPU:0 before, /device:TPU:103 now
where the time goes in v2:
time: 165 us; the launch traced here: 163 us
  starting transfers between devices  62.2 us (38%)
  waiting for transfers between devices  46.5 us (28%)
  Pallas kernels  30.2 us (18%)
  local copies, waits for them, and re-layouts  14.3 us (9%)
  other arithmetic  8.82 us (5%)
    ppermute x32, starting transfers between devices, ring(): return lax.ppermute(value, axis, [(i, (i + step) % N) for i in range(N)])  48.4 us
    ppermute x32, waiting for transfers between devices, ring(): return lax.ppermute(value, axis, [(i, (i + step) % N) for i in range(N)])  38.5 us
    pallas_call x5, Pallas kernels, call(): pl.pallas_call(kernel, name=name, out_shape=shapes, in_specs=[pl.BlockSpe...  30.2 us
    all_to_all x2, starting transfers between devices, everyone(): return lax.all_to_all(copies, axis, 0, 0)  13.8 us
    all_to_all x2, waiting for transfers between devices, everyone(): return lax.all_to_all(copies, axis, 0, 0)  8.02 us
  transfers between devices with their start and end apart: 34, of which 16 were waited for; matrix products, arithmetic and copies ran while one was open for 10% of the time, Pallas kernels for 9%

profile of v2, /device:TPU:103, one launch (start us, length us, event | category | flops | bytes accessed | tf_op | source)
XLA Modules:
  0.0 162.8 jit_solution(2530305573263896399)
XLA Ops:
  0.0 1.3 slice_bitcast_fusion.2
  4.8 3.0 %collective-permute-start.4 = (f32[1944,128]{1,0:T(8,128)}, f32[1944,128]{1,0:T(8,128)}, u32[]{:S(2)}, u32[]{:S(2)}) collective-permute-start(f32[1944,128]{1,0:T(8,128)} %maximum_maximum_fusion), channel_id=1, source_target_pairs={{0,16},{16,32},{32,48},{48,64},{64,80},{80,96},{96,112},{112,128},... | collective-permute-start | bytes 2985992 | tf_op jit(solution)/shard_map/two_three_halo/ppermute | solution.py:16
  7.8 5.1 %collective-permute-done.xlo = f32[2,7,32,256]{3,2,1,0:T(8,128)S(1)} collective-permute-done((f32[2,7,32,256]{3,2,1,0:T(8,128)S(1)}, f32[2,7,32,256]{3,2,1,0:T(8,128)S(1)}, u32[]{:S(2)}, u32[]{:S(2)}) %collective-permute-start) | collective-permute-done | bytes 458784 | tf_op jit(solution)/shard_map/fine_halo/ppermute | solution.py:16
  12.9 3.1 %collective-permute-done.1.xhi = f32[2,7,32,256]{3,2,1,0:T(8,128)S(1)} collective-permute-done((f32[2,7,32,256]{3,2,1,0:T(8,128)S(1)}, f32[2,7,32,256]{3,2,1,0:T(8,128)S(1)}, u32[]{:S(2)}, u32[]{:S(2)}) %collective-permute-start.1) | collective-permute-done | bytes 458784 | tf_op jit(solution)/shard_map/fine_halo/ppermute | solution.py:16
  16.1 6.1 %collective-permute-start.2 = (f32[2,22,8,256]{3,2,1,0:T(8,128)S(1)}, f32[2,22,8,256]{3,2,1,0:T(8,128)S(1)}, u32[]{:S(2)}, u32[]{:S(2)}) collective-permute-start(f32[2,22,8,256]{3,2,1,0:T(8,128)S(1)} %pad_maximum_fusion.11), channel_id=1, source_target_pairs={{0,1},{1,2},{2,3},{3,4},{4,5},{5,6},{6,7},{7,8},{8,9},{9,10},{10,1... | collective-permute-start | bytes 1081352 | tf_op jit(solution)/shard_map/fine_halo/ppermute | solution.py:16
  24.0 3.0 %collective-permute-start.6 = (f32[27,4,8,128]{3,2,1,0:T(8,128)}, f32[27,4,8,128]{3,2,1,0:T(8,128)}, u32[]{:S(2)}, u32[]{:S(2)}) collective-permute-start(f32[27,4,8,128]{3,2,1,0:T(8,128)} %get-tuple-element.84), channel_id=1, source_target_pairs={{0,1},{1,2},{2,3},{3,4},{4,5},{5,6},{6,7},{7,8},{8,9},{9,10},{10,1... | collective-permute-start | bytes 1327112 | tf_op jit(solution)/shard_map/fine_halo/ppermute | solution.py:16
  27.1 10.4 %collective-permute-done.3.yhi = f32[2,22,8,256]{3,2,1,0:T(8,128)S(1)} collective-permute-done((f32[2,22,8,256]{3,2,1,0:T(8,128)}, f32[2,22,8,256]{3,2,1,0:T(8,128)S(1)}, u32[]{:S(2)}, u32[]{:S(2)}) %collective-permute-start.3) | collective-permute-done | bytes 360480 | tf_op jit(solution)/shard_map/fine_halo/ppermute | solution.py:16
  37.4 6.6 %fine_down.1 = (f32[16,48,256]{2,1,0:T(8,128)S(1)}, f32[6,16,128]{2,1,0:T(8,128)S(1)}, f32[16,48,256]{2,1,0:T(8,128)S(1)}, f32[16,48,256]{2,1,0:T(8,128)}) custom-call(s32[2]{0:T(128)S(1)} %pad_add_fusion.pos, f32[8,32,256]{2,1,0:T(8,128)S(1)} %copy-done.7, f32[8,32,256]{2,1,0:T(8,128)S(1)} %copy-done.8, f32[2,7,32,256]{3,2,1,0:T(8,128)S(1)} %collective-permute-done.xlo, ...), custom_call_target="tpu_custom_call" | custom-call | tf_op jit(solution)/shard_map/fine_down/fine_down/pallas_call | solution.py:501
  44.9 1.5 collective-permute-start.9
  50.2 2.9 %collective-permute-start.10 = (f32[1840,128]{1,0:T(8,128)S(1)}, f32[1840,128]{1,0:T(8,128)S(1)}, u32[]{:S(2)}, u32[]{:S(2)}) collective-permute-start(f32[1840,128]{1,0:T(8,128)S(1)} %pad_maximum_fusion.3), channel_id=1, source_target_pairs={{0,1},{1,2},{2,3},{3,4},{4,5},{5,6},{6,7},{7,8},{8,9},{9,10},{10,1... | collective-permute-start | bytes 2826248 | tf_op jit(solution)/shard_map/one_exchange/ppermute | solution.py:16
  55.1 2.8 %collective-permute-start.15 = (f32[2,216,128]{2,1,0:T(8,128)S(1)}, f32[2,216,128]{2,1,0:T(8,128)S(1)}, u32[]{:S(2)}, u32[]{:S(2)}) collective-permute-start(f32[2,216,128]{2,1,0:T(8,128)S(1)} %get-tuple-element.101), channel_id=1, source_target_pairs={{0,208},{16,224},{32,240},{48,0},{64,16},{80,32},{96,48},{112,64},... | collective-permute-start | bytes 663560 | tf_op jit(solution)/shard_map/two_halo/ppermute | solution.py:16
  57.9 1.7 %pad_maximum_fusion.cx = f32[27,12,16,128]{3,2,1,0:T(8,128)} fusion(f32[27,4,16,128]{3,2,1,0:T(8,128)S(1)} %bitcast.87, f32[27,4,16,128]{3,2,1,0:T(8,128)S(1)} %copy-done.16, f32[27,4,16,128]{3,2,1,0:T(8,128)S(1)} %bitcast.85), kind=kLoop, calls=%fused_computation | loop fusion | flops 1327104 | bytes 5308416 | tf_op jit(solution)/shard_map/one_down/concatenate | solution.py:598
  59.6 4.8 %collective-permute-done.11 = f32[1840,128]{1,0:T(8,128)S(1)} collective-permute-done((f32[1840,128]{1,0:T(8,128)S(1)}, f32[1840,128]{1,0:T(8,128)S(1)}, u32[]{:S(2)}, u32[]{:S(2)}) %collective-permute-start.11) | collective-permute-done | bytes 942112 | tf_op jit(solution)/shard_map/one_exchange/ppermute | solution.py:16
  64.9 2.9 %collective-permute-start.16 = (f32[7,216,128]{2,1,0:T(8,128)S(1)}, f32[7,216,128]{2,1,0:T(8,128)S(1)}, u32[]{:S(2)}, u32[]{:S(2)}) collective-permute-start(f32[7,216,128]{2,1,0:T(8,128)S(1)} %constant_dynamic-update-slice_fusion.c2own), channel_id=1, source_target_pairs={{0,1},{1,2},{2,3},{3,4},{4,5},{5,6},{6,7},{7,8},{8,9},{9,10},{10,1... | collective-permute-start | bytes 2322440 | tf_op jit(solution)/shard_map/two_halo/ppermute | solution.py:16
  69.3 1.4 pad_maximum_fusion.1.clo
  70.8 5.9 %one_down.1 = (f32[8,128]{1,0:T(8,128)S(1)}, f32[4,16,128]{2,1,0:T(8,128)S(1)}) custom-call(s32[2]{0:T(128)S(1)} %pad_add_fusion.pos, f32[14,32,128]{2,1,0:T(8,128)S(1)} %pad_maximum_fusion.13.g.g1, f32[27,12,16,128]{3,2,1,0:T(8,128)} %pad_maximum_fusion.cx, f32[27,12,8,128]{3,2,1,0:T(8,128)S(1)} %pad_maximum_fusion.1.clo, ...), custom_call_target="tpu_custom_call" | custom-call | tf_op jit(solution)/shard_map/one_down/one_down/pallas_call | solution.py:501
  76.7 3.0 %collective-permute-start.12 = (f32[8,128]{1,0:T(8,128)S(1)}, f32[8,128]{1,0:T(8,128)S(1)}, u32[]{:S(2)}, u32[]{:S(2)}) collective-permute-start(f32[8,128]{1,0:T(8,128)S(1)} %get-tuple-element.56), channel_id=1, source_target_pairs={{0,1},{1,2},{2,3},{3,4},{4,5},{5,6},{6,7},{7,8},{8,9},{9,10},{10,1... | collective-permute-start | bytes 12296 | tf_op jit(solution)/shard_map/two_exchange/ppermute | solution.py:16
  83.5 7.4 %all-to-all-start = ((f32[16,56,128]{2,1,0:T(8,128)}), f32[16,56,128]{2,1,0:T(8,128)S(1)}, u32[]{:S(2)}, u32[]{:S(2)}) async-start(f32[16,56,128]{2,1,0:T(8,128)} %broadcast_in_dim.4), calls=%async_computation | async-start | bytes 917504 | tf_op jit(solution)/shard_map/two_exchange/all_to_all | solution.py:21
  91.5 3.0 %collective-permute-start.20 = (f32[4,16,128]{2,1,0:T(8,128)S(1)}, f32[4,16,128]{2,1,0:T(8,128)S(1)}, u32[]{:S(2)}, u32[]{:S(2)}) collective-permute-start(f32[4,16,128]{2,1,0:T(8,128)S(1)} %get-tuple-element.67), channel_id=1, source_target_pairs={{0,16},{16,32},{32,48},{48,64},{64,80},{80,96},{96,112},{112,128},... | collective-permute-start | bytes 98312 | tf_op jit(solution)/shard_map/one_values/ppermute | solution.py:16
  94.5 3.1 %all-to-all-done.g_all.g2_all = f32[16,56,128]{2,1,0:T(8,128)S(1)} async-done(((f32[16,56,128]{2,1,0:T(8,128)}), f32[16,56,128]{2,1,0:T(8,128)S(1)}, u32[]{:S(2)}, u32[]{:S(2)}) %all-to-all-start) | async-done | bytes 458784 | tf_op jit(solution)/shard_map/two_exchange/all_to_all | solution.py:21
  98.8 1.7 %two_down.1 = (f32[8,128]{1,0:T(8,128)S(1)}, f32[8,128]{1,0:T(8,128)S(1)}) custom-call(s32[2]{0:T(128)S(1)} %pad_add_fusion.pos, f32[16,56,128]{2,1,0:T(8,128)S(1)} %all-to-all-done.g_all.g2_all, f32[7,216,128]{2,1,0:T(8,128)S(1)} %copy-done.6, f32[7,216,128]{2,1,0:T(8,128)S(1)} %constant_dynamic-update-slice_fusion.c2own, f32[7,216,128]{2,1,0:T(8,128)S(1)} %copy-done.4), custom_call_target="tpu_custom_call" | custom-call | tf_op jit(solution)/shard_map/two_down/two_down/pallas_call | solution.py:501
  100.9 4.0 %collective-permute-start.18 = (f32[432,128]{1,0:T(8,128)S(1)}, f32[432,128]{1,0:T(8,128)S(1)}, u32[]{:S(2)}, u32[]{:S(2)}) collective-permute-start(f32[432,128]{1,0:T(8,128)S(1)} %bitcast.100), channel_id=1, source_target_pairs={{0,1},{1,2},{2,3},{3,4},{4,5},{5,6},{6,7},{7,8},{8,9},{9,10},{10,1... | collective-permute-start | bytes 663560 | tf_op jit(solution)/shard_map/three_halo/ppermute | solution.py:16
  106.5 1.9 %collective-permute-done.22 = f32[112,128]{1,0:T(8,128)S(1)} collective-permute-done((f32[112,128]{1,0:T(8,128)S(1)}, f32[112,128]{1,0:T(8,128)S(1)}, u32[]{:S(2)}, u32[]{:S(2)}) %collective-permute-start.22) | collective-permute-done | bytes 57376 | tf_op jit(solution)/shard_map/three_exchange/ppermute | solution.py:16
  109.0 2.7 %collective-permute-start.24 = (f32[3,128]{1,0:T(4,128)S(1)}, f32[3,128]{1,0:T(4,128)S(1)}, u32[]{:S(2)}, u32[]{:S(2)}) collective-permute-start(f32[3,128]{1,0:T(4,128)S(1)} %pad_maximum_fusion.23), channel_id=1, source_target_pairs={{0,2},{1,3},{2,4},{3,5},{4,6},{5,7},{6,8},{7,9},{8,10},{9,11},{10,... | collective-permute-start | bytes 4616 | tf_op jit(solution)/shard_map/three_exchange/ppermute | solution.py:16
  114.9 6.4 %all-to-all-start.1 = ((f32[16,32,128]{2,1,0:T(8,128)}), f32[16,32,128]{2,1,0:T(8,128)}, u32[]{:S(2)}, u32[]{:S(2)}) async-start(f32[16,32,128]{2,1,0:T(8,128)} %broadcast_in_dim.5), calls=%async_computation.1 | async-start | bytes 524288 | tf_op jit(solution)/shard_map/three_exchange/all_to_all | solution.py:21
  121.9 4.9 %all-to-all-done.1 = f32[16,32,128]{2,1,0:T(8,128)} async-done(((f32[16,32,128]{2,1,0:T(8,128)}), f32[16,32,128]{2,1,0:T(8,128)}, u32[]{:S(2)}, u32[]{:S(2)}) %all-to-all-start.1) | async-done | bytes 262176 | tf_op jit(solution)/shard_map/three_exchange/all_to_all | solution.py:21
  128.7 10.9 %coarse_up.1 = f32[4,16,128]{2,1,0:T(8,128)S(1)} custom-call(s32[2]{0:T(128)S(1)} %pad_add_fusion.pos, f32[7,16,128]{2,1,0:T(8,128)S(1)} %copy.19.g3, f32[16,24,128]{2,1,0:T(8,128)S(1)} %slice.272.v2, f32[2,27,16,128]{3,2,1,0:T(8,128)S(1)} %bitcast.82, f32[3,27,16,128]{3,2,1,0:T(8,128)S(1)} %copy.20.c3own, f32[2,27,16,128]{3,2,1,0:T(8,128)S(1)} %bitcast.83, ...), custom_call_target="tpu_custom_call" | custom-call | tf_op jit(solution)/shard_map/coarse_up/coarse_up/pallas_call | solution.py:501
  139.6 1.7 %collective-permute-start.28 = (f32[3,16,128]{2,1,0:T(8,128)S(1)}, f32[3,16,128]{2,1,0:T(8,128)S(1)}, u32[]{:S(2)}, u32[]{:S(2)}) collective-permute-start(f32[3,16,128]{2,1,0:T(8,128)S(1)} %get-tuple-element.119), channel_id=1, source_target_pairs={{0,16},{16,32},{32,48},{48,64},{64,80},{80,96},{96,112},{112,128},... | collective-permute-start | bytes 73736 | tf_op jit(solution)/shard_map/one_back/ppermute | solution.py:16
  142.4 3.7 %collective-permute-done.29 = f32[3,16,128]{2,1,0:T(8,128)S(1)} collective-permute-done((f32[3,16,128]{2,1,0:T(8,128)S(1)}, f32[3,16,128]{2,1,0:T(8,128)S(1)}, u32[]{:S(2)}, u32[]{:S(2)}) %collective-permute-start.29) | collective-permute-done | bytes 24608 | tf_op jit(solution)/shard_map/one_back/ppermute | solution.py:16
  146.1 6.8 %collective-permute-start.30 = (f32[10,8,128]{2,1,0:T(8,128)S(1)}, f32[10,8,128]{2,1,0:T(8,128)S(1)}, u32[]{:S(2)}, u32[]{:S(2)}) collective-permute-start(f32[10,8,128]{2,1,0:T(8,128)S(1)} %get-tuple-element.111), channel_id=1, source_target_pairs={{0,1},{1,2},{2,3},{3,4},{4,5},{5,6},{6,7},{7,8},{8,9},{9,10},{10,1... | collective-permute-start | bytes 122888 | tf_op jit(solution)/shard_map/one_back/ppermute | solution.py:16
  154.0 3.5 %collective-permute-done.31 = f32[10,8,128]{2,1,0:T(8,128)S(1)} collective-permute-done((f32[10,8,128]{2,1,0:T(8,128)S(1)}, f32[10,8,128]{2,1,0:T(8,128)S(1)}, u32[]{:S(2)}, u32[]{:S(2)}) %collective-permute-start.31) | collective-permute-done | bytes 40992 | tf_op jit(solution)/shard_map/one_back/ppermute | solution.py:16
  157.6 5.1 %fine_up.1 = f32[8,32,256]{2,1,0:T(8,128)} custom-call(s32[2]{0:T(128)S(1)} %pad_add_fusion.pos, f32[16,48,256]{2,1,0:T(8,128)S(1)} %copy-done.14, f32[16,48,256]{2,1,0:T(8,128)S(1)} %copy-done.15, f32[16,48,256]{2,1,0:T(8,128)S(1)} %copy-done.12, f32[10,32,128]{2,1,0:T(8,128)S(1)} %pad_maximum_fusion.15.c1), custom_call_target="tpu_custom_call" | custom-call | tf_op jit(solution)/shard_map/fine_up/fine_up/pallas_call | solution.py:501
  (167 shorter events, 29.6 us)
Async XLA Ops:
  1.4 11.5 %collective-permute-start = (f32[2,7,32,256]{3,2,1,0:T(8,128)S(1)}, f32[2,7,32,256]{3,2,1,0:T(8,128)S(1)}, u32[]{:S(2)}, u32[]{:S(2)}) collective-permute-start(f32[2,7,32,256]{3,2,1,0:T(8,128)S(1)} %pad_maximum_fusion.7), channel_id=1, source_target_pairs={{0,16},{16,32},{32,48},{48,64},{64,80},{80,96},{96,112},{112,128},... | collective-permute-start | bytes 1376264 | tf_op jit(solution)/shard_map/fine_halo/ppermute | solution.py:16
  2.8 13.3 %collective-permute-start.1 = (f32[2,7,32,256]{3,2,1,0:T(8,128)S(1)}, f32[2,7,32,256]{3,2,1,0:T(8,128)S(1)}, u32[]{:S(2)}, u32[]{:S(2)}) collective-permute-start(f32[2,7,32,256]{3,2,1,0:T(8,128)S(1)} %pad_maximum_fusion.8), channel_id=1, source_target_pairs={{0,240},{16,0},{32,16},{48,32},{64,48},{80,64},{96,80},{112,96},{1... | collective-permute-start | bytes 1376264 | tf_op jit(solution)/shard_map/fine_halo/ppermute | solution.py:16
  4.2 39.8 %collective-permute-start.5 = (f32[1944,128]{1,0:T(8,128)}, f32[1944,128]{1,0:T(8,128)}, u32[]{:S(2)}, u32[]{:S(2)}) collective-permute-start(f32[1944,128]{1,0:T(8,128)} %maximum_maximum_fusion), channel_id=1, source_target_pairs={{0,240},{16,0},{32,16},{48,32},{64,48},{80,64},{96,80},{112,96},{1... | collective-permute-start | bytes 2985992 | tf_op jit(solution)/shard_map/two_three_halo/ppermute | solution.py:16
  4.8 39.2 %collective-permute-start.4 = (f32[1944,128]{1,0:T(8,128)}, f32[1944,128]{1,0:T(8,128)}, u32[]{:S(2)}, u32[]{:S(2)}) collective-permute-start(f32[1944,128]{1,0:T(8,128)} %maximum_maximum_fusion), channel_id=1, source_target_pairs={{0,16},{16,32},{32,48},{48,64},{64,80},{80,96},{96,112},{112,128},... | collective-permute-start | bytes 2985992 | tf_op jit(solution)/shard_map/two_three_halo/ppermute | solution.py:16
  16.1 10.9 %collective-permute-start.2 = (f32[2,22,8,256]{3,2,1,0:T(8,128)S(1)}, f32[2,22,8,256]{3,2,1,0:T(8,128)S(1)}, u32[]{:S(2)}, u32[]{:S(2)}) collective-permute-start(f32[2,22,8,256]{3,2,1,0:T(8,128)S(1)} %pad_maximum_fusion.11), channel_id=1, source_target_pairs={{0,1},{1,2},{2,3},{3,4},{4,5},{5,6},{6,7},{7,8},{8,9},{9,10},{10,1... | collective-permute-start | bytes 1081352 | tf_op jit(solution)/shard_map/fine_halo/ppermute | solution.py:16
  24.0 20.0 %collective-permute-start.7 = (f32[27,4,8,128]{3,2,1,0:T(8,128)}, f32[27,4,8,128]{3,2,1,0:T(8,128)}, u32[]{:S(2)}, u32[]{:S(2)}) collective-permute-start(f32[27,4,8,128]{3,2,1,0:T(8,128)} %get-tuple-element.83), channel_id=1, source_target_pairs={{0,15},{1,0},{2,1},{3,2},{4,3},{5,4},{6,5},{7,6},{8,7},{9,8},{10,9... | collective-permute-start | bytes 1327112 | tf_op jit(solution)/shard_map/fine_halo/ppermute | solution.py:16
  24.0 20.0 %collective-permute-start.6 = (f32[27,4,8,128]{3,2,1,0:T(8,128)}, f32[27,4,8,128]{3,2,1,0:T(8,128)}, u32[]{:S(2)}, u32[]{:S(2)}) collective-permute-start(f32[27,4,8,128]{3,2,1,0:T(8,128)} %get-tuple-element.84), channel_id=1, source_target_pairs={{0,1},{1,2},{2,3},{3,4},{4,5},{5,6},{6,7},{7,8},{8,9},{9,10},{10,1... | collective-permute-start | bytes 1327112 | tf_op jit(solution)/shard_map/fine_halo/ppermute | solution.py:16
  27.0 10.5 %collective-permute-start.3 = (f32[2,22,8,256]{3,2,1,0:T(8,128)}, f32[2,22,8,256]{3,2,1,0:T(8,128)S(1)}, u32[]{:S(2)}, u32[]{:S(2)}) collective-permute-start(f32[2,22,8,256]{3,2,1,0:T(8,128)} %pad_maximum_fusion.12), channel_id=1, source_target_pairs={{0,15},{1,0},{2,1},{3,2},{4,3},{5,4},{6,5},{7,6},{8,7},{9,8},{10,9... | collective-permute-start | bytes 1081352 | tf_op jit(solution)/shard_map/fine_halo/ppermute | solution.py:16
  44.9 4.2 %collective-permute-start.8 = (f32[5,16,128]{2,1,0:T(8,128)S(1)}, f32[5,16,128]{2,1,0:T(8,128)S(1)}, u32[]{:S(2)}, u32[]{:S(2)}) collective-permute-start(f32[5,16,128]{2,1,0:T(8,128)S(1)} %get-tuple-element.121), channel_id=1, source_target_pairs={{0,16},{16,32},{32,48},{48,64},{64,80},{80,96},{96,112},{112,128},... | collective-permute-start | bytes 122888 | tf_op jit(solution)/shard_map/one_exchange/ppermute | solution.py:16
  44.9 5.0 %collective-permute-start.9 = (f32[5,16,128]{2,1,0:T(8,128)S(1)}, f32[5,16,128]{2,1,0:T(8,128)S(1)}, u32[]{:S(2)}, u32[]{:S(2)}) collective-permute-start(f32[5,16,128]{2,1,0:T(8,128)S(1)} %get-tuple-element.122), channel_id=1, source_target_pairs={{0,240},{16,0},{32,16},{48,32},{64,48},{80,64},{96,80},{112,96},{1... | collective-permute-start | bytes 122888 | tf_op jit(solution)/shard_map/one_exchange/ppermute | solution.py:16
  50.1 14.3 %collective-permute-start.11 = (f32[1840,128]{1,0:T(8,128)S(1)}, f32[1840,128]{1,0:T(8,128)S(1)}, u32[]{:S(2)}, u32[]{:S(2)}) collective-permute-start(f32[1840,128]{1,0:T(8,128)S(1)} %pad_maximum_fusion.4), channel_id=1, source_target_pairs={{0,15},{1,0},{2,1},{3,2},{4,3},{5,4},{6,5},{7,6},{8,7},{9,8},{10,9... | collective-permute-start | bytes 2826248 | tf_op jit(solution)/shard_map/one_exchange/ppermute | solution.py:16
  50.2 14.2 %collective-permute-start.10 = (f32[1840,128]{1,0:T(8,128)S(1)}, f32[1840,128]{1,0:T(8,128)S(1)}, u32[]{:S(2)}, u32[]{:S(2)}) collective-permute-start(f32[1840,128]{1,0:T(8,128)S(1)} %pad_maximum_fusion.3), channel_id=1, source_target_pairs={{0,1},{1,2},{2,3},{3,4},{4,5},{5,6},{6,7},{7,8},{8,9},{9,10},{10,1... | collective-permute-start | bytes 2826248 | tf_op jit(solution)/shard_map/one_exchange/ppermute | solution.py:16
  55.1 9.3 %collective-permute-start.15 = (f32[2,216,128]{2,1,0:T(8,128)S(1)}, f32[2,216,128]{2,1,0:T(8,128)S(1)}, u32[]{:S(2)}, u32[]{:S(2)}) collective-permute-start(f32[2,216,128]{2,1,0:T(8,128)S(1)} %get-tuple-element.101), channel_id=1, source_target_pairs={{0,208},{16,224},{32,240},{48,0},{64,16},{80,32},{96,48},{112,64},... | collective-permute-start | bytes 663560 | tf_op jit(solution)/shard_map/two_halo/ppermute | solution.py:16
  57.9 6.7 %collective-permute-start.14 = (f32[2,216,128]{2,1,0:T(8,128)S(1)}, f32[2,216,128]{2,1,0:T(8,128)S(1)}, u32[]{:S(2)}, u32[]{:S(2)}) collective-permute-start(f32[2,216,128]{2,1,0:T(8,128)S(1)} %get-tuple-element.102), channel_id=1, source_target_pairs={{0,48},{16,64},{32,80},{48,96},{64,112},{80,128},{96,144},{112,160... | collective-permute-start | bytes 663560 | tf_op jit(solution)/shard_map/two_halo/ppermute | solution.py:16
  64.8 16.1 %collective-permute-start.17 = (f32[7,216,128]{2,1,0:T(8,128)S(1)}, f32[7,216,128]{2,1,0:T(8,128)S(1)}, u32[]{:S(2)}, u32[]{:S(2)}) collective-permute-start(f32[7,216,128]{2,1,0:T(8,128)S(1)} %constant_dynamic-update-slice_fusion.c2own), channel_id=1, source_target_pairs={{0,15},{1,0},{2,1},{3,2},{4,3},{5,4},{6,5},{7,6},{8,7},{9,8},{10,9... | collective-permute-start | bytes 2322440 | tf_op jit(solution)/shard_map/two_halo/ppermute | solution.py:16
  64.9 17.0 %collective-permute-start.16 = (f32[7,216,128]{2,1,0:T(8,128)S(1)}, f32[7,216,128]{2,1,0:T(8,128)S(1)}, u32[]{:S(2)}, u32[]{:S(2)}) collective-permute-start(f32[7,216,128]{2,1,0:T(8,128)S(1)} %constant_dynamic-update-slice_fusion.c2own), channel_id=1, source_target_pairs={{0,1},{1,2},{2,3},{3,4},{4,5},{5,6},{6,7},{7,8},{8,9},{9,10},{10,1... | collective-permute-start | bytes 2322440 | tf_op jit(solution)/shard_map/two_halo/ppermute | solution.py:16
  76.7 4.3 %collective-permute-start.13 = (f32[8,128]{1,0:T(8,128)S(1)}, f32[8,128]{1,0:T(8,128)S(1)}, u32[]{:S(2)}, u32[]{:S(2)}) collective-permute-start(f32[8,128]{1,0:T(8,128)S(1)} %get-tuple-element.56), channel_id=1, source_target_pairs={{0,15},{1,0},{2,1},{3,2},{4,3},{5,4},{6,5},{7,6},{8,7},{9,8},{10,9... | collective-permute-start | bytes 12296 | tf_op jit(solution)/shard_map/two_exchange/ppermute | solution.py:16
  76.7 4.3 %collective-permute-start.12 = (f32[8,128]{1,0:T(8,128)S(1)}, f32[8,128]{1,0:T(8,128)S(1)}, u32[]{:S(2)}, u32[]{:S(2)}) collective-permute-start(f32[8,128]{1,0:T(8,128)S(1)} %get-tuple-element.56), channel_id=1, source_target_pairs={{0,1},{1,2},{2,3},{3,4},{4,5},{5,6},{6,7},{7,8},{8,9},{9,10},{10,1... | collective-permute-start | bytes 12296 | tf_op jit(solution)/shard_map/two_exchange/ppermute | solution.py:16
  83.5 14.1 %all-to-all-start = ((f32[16,56,128]{2,1,0:T(8,128)}), f32[16,56,128]{2,1,0:T(8,128)S(1)}, u32[]{:S(2)}, u32[]{:S(2)}) async-start(f32[16,56,128]{2,1,0:T(8,128)} %broadcast_in_dim.4), calls=%async_computation | async-start | bytes 917504 | tf_op jit(solution)/shard_map/two_exchange/all_to_all | solution.py:21
  91.0 9.5 %collective-permute-start.21 = (f32[4,16,128]{2,1,0:T(8,128)S(1)}, f32[4,16,128]{2,1,0:T(8,128)S(1)}, u32[]{:S(2)}, u32[]{:S(2)}) collective-permute-start(f32[4,16,128]{2,1,0:T(8,128)S(1)} %get-tuple-element.67), channel_id=1, source_target_pairs={{0,240},{16,0},{32,16},{48,32},{64,48},{80,64},{96,80},{112,96},{1... | collective-permute-start | bytes 98312 | tf_op jit(solution)/shard_map/one_values/ppermute | solution.py:16
  91.5 9.0 %collective-permute-start.20 = (f32[4,16,128]{2,1,0:T(8,128)S(1)}, f32[4,16,128]{2,1,0:T(8,128)S(1)}, u32[]{:S(2)}, u32[]{:S(2)}) collective-permute-start(f32[4,16,128]{2,1,0:T(8,128)S(1)} %get-tuple-element.67), channel_id=1, source_target_pairs={{0,16},{16,32},{32,48},{48,64},{64,80},{80,96},{96,112},{112,128},... | collective-permute-start | bytes 98312 | tf_op jit(solution)/shard_map/one_values/ppermute | solution.py:16
  100.6 5.9 %collective-permute-start.23 = (f32[112,128]{1,0:T(8,128)S(1)}, f32[112,128]{1,0:T(8,128)S(1)}, u32[]{:S(2)}, u32[]{:S(2)}) collective-permute-start(f32[112,128]{1,0:T(8,128)S(1)} %get-tuple-element.123), channel_id=1, source_target_pairs={{0,15},{1,0},{2,1},{3,2},{4,3},{5,4},{6,5},{7,6},{8,7},{9,8},{10,9... | collective-permute-start | bytes 172040 | tf_op jit(solution)/shard_map/three_exchange/ppermute | solution.py:16
  100.8 8.0 %collective-permute-start.19 = (f32[432,128]{1,0:T(8,128)S(1)}, f32[432,128]{1,0:T(8,128)S(1)}, u32[]{:S(2)}, u32[]{:S(2)}) collective-permute-start(f32[432,128]{1,0:T(8,128)S(1)} %bitcast.99), channel_id=1, source_target_pairs={{0,15},{1,0},{2,1},{3,2},{4,3},{5,4},{6,5},{7,6},{8,7},{9,8},{10,9... | collective-permute-start | bytes 663560 | tf_op jit(solution)/shard_map/three_halo/ppermute | solution.py:16
  100.9 8.0 %collective-permute-start.18 = (f32[432,128]{1,0:T(8,128)S(1)}, f32[432,128]{1,0:T(8,128)S(1)}, u32[]{:S(2)}, u32[]{:S(2)}) collective-permute-start(f32[432,128]{1,0:T(8,128)S(1)} %bitcast.100), channel_id=1, source_target_pairs={{0,1},{1,2},{2,3},{3,4},{4,5},{5,6},{6,7},{7,8},{8,9},{9,10},{10,1... | collective-permute-start | bytes 663560 | tf_op jit(solution)/shard_map/three_halo/ppermute | solution.py:16
  108.9 5.2 %collective-permute-start.25 = (f32[3,128]{1,0:T(4,128)S(1)}, f32[3,128]{1,0:T(4,128)S(1)}, u32[]{:S(2)}, u32[]{:S(2)}) collective-permute-start(f32[3,128]{1,0:T(4,128)S(1)} %pad_maximum_fusion.23), channel_id=1, source_target_pairs={{0,14},{1,15},{2,0},{3,1},{4,2},{5,3},{6,4},{7,5},{8,6},{9,7},{10,... | collective-permute-start | bytes 4616 | tf_op jit(solution)/shard_map/three_exchange/ppermute | solution.py:16
  109.0 5.1 %collective-permute-start.24 = (f32[3,128]{1,0:T(4,128)S(1)}, f32[3,128]{1,0:T(4,128)S(1)}, u32[]{:S(2)}, u32[]{:S(2)}) collective-permute-start(f32[3,128]{1,0:T(4,128)S(1)} %pad_maximum_fusion.23), channel_id=1, source_target_pairs={{0,2},{1,3},{2,4},{3,5},{4,6},{5,7},{6,8},{7,9},{8,10},{9,11},{10,... | collective-permute-start | bytes 4616 | tf_op jit(solution)/shard_map/three_exchange/ppermute | solution.py:16
  112.6 16.0 %collective-permute-start.26 = (f32[864,128]{1,0:T(8,128)}, f32[864,128]{1,0:T(8,128)S(1)}, u32[]{:S(2)}, u32[]{:S(2)}) collective-permute-start(f32[864,128]{1,0:T(8,128)} %bitcast.39), channel_id=1, source_target_pairs={{0,2},{1,3},{2,4},{3,5},{4,6},{5,7},{6,8},{7,9},{8,10},{9,11},{10,... | collective-permute-start | bytes 1327112 | tf_op jit(solution)/shard_map/three_exchange/ppermute | solution.py:16
  113.2 15.5 %collective-permute-start.27 = (f32[864,128]{1,0:T(8,128)}, f32[864,128]{1,0:T(8,128)S(1)}, u32[]{:S(2)}, u32[]{:S(2)}) collective-permute-start(f32[864,128]{1,0:T(8,128)} %bitcast.41), channel_id=1, source_target_pairs={{0,14},{1,15},{2,0},{3,1},{4,2},{5,3},{6,4},{7,5},{8,6},{9,7},{10,... | collective-permute-start | bytes 1327112 | tf_op jit(solution)/shard_map/three_exchange/ppermute | solution.py:16
  114.9 12.0 %all-to-all-start.1 = ((f32[16,32,128]{2,1,0:T(8,128)}), f32[16,32,128]{2,1,0:T(8,128)}, u32[]{:S(2)}, u32[]{:S(2)}) async-start(f32[16,32,128]{2,1,0:T(8,128)} %broadcast_in_dim.5), calls=%async_computation.1 | async-start | bytes 524288 | tf_op jit(solution)/shard_map/three_exchange/all_to_all | solution.py:21
  141.3 4.8 %collective-permute-start.29 = (f32[3,16,128]{2,1,0:T(8,128)S(1)}, f32[3,16,128]{2,1,0:T(8,128)S(1)}, u32[]{:S(2)}, u32[]{:S(2)}) collective-permute-start(f32[3,16,128]{2,1,0:T(8,128)S(1)} %get-tuple-element.120), channel_id=1, source_target_pairs={{0,240},{16,0},{32,16},{48,32},{64,48},{80,64},{96,80},{112,96},{1... | collective-permute-start | bytes 73736 | tf_op jit(solution)/shard_map/one_back/ppermute | solution.py:16
  146.1 7.9 %collective-permute-start.30 = (f32[10,8,128]{2,1,0:T(8,128)S(1)}, f32[10,8,128]{2,1,0:T(8,128)S(1)}, u32[]{:S(2)}, u32[]{:S(2)}) collective-permute-start(f32[10,8,128]{2,1,0:T(8,128)S(1)} %get-tuple-element.111), channel_id=1, source_target_pairs={{0,1},{1,2},{2,3},{3,4},{4,5},{5,6},{6,7},{7,8},{8,9},{9,10},{10,1... | collective-permute-start | bytes 122888 | tf_op jit(solution)/shard_map/one_back/ppermute | solution.py:16
  152.9 4.6 %collective-permute-start.31 = (f32[10,8,128]{2,1,0:T(8,128)S(1)}, f32[10,8,128]{2,1,0:T(8,128)S(1)}, u32[]{:S(2)}, u32[]{:S(2)}) collective-permute-start(f32[10,8,128]{2,1,0:T(8,128)S(1)} %get-tuple-element.112), channel_id=1, source_target_pairs={{0,15},{1,0},{2,1},{3,2},{4,3},{5,4},{6,5},{7,6},{8,7},{9,8},{10,9... | collective-permute-start | bytes 122888 | tf_op jit(solution)/shard_map/one_back/ppermute | solution.py:16
  (27 other events, 309.6 us)

commit v3 on v2

--- a/solution.py
+++ b/solution.py
@@ -590,9 +590,6 @@
         tlo, thi = lax.optimization_barrier((tlo, thi, before, after))[:2]
         far_lo = ring(jnp.stack([c2, thi]), "gx", 3)
         far_hi = ring(jnp.stack([tlo, c2]), "gx", -3)
-        far_lo, far_hi = lax.optimization_barrier((far_lo, far_hi, g1e))[:2]
-        c2own = jnp.concatenate([far_lo, tlo[None], c2[None], thi[None], far_hi])
-        c2lo, c2hi = ring(c2own, "gy", 1), ring(c2own, "gy", -1)
 
     with jax.named_scope("one_down"):
         cx = jnp.concatenate([after_all(cxlo, before), coarse_one, cxhi], axis=1)
@@ -606,7 +603,10 @@
 
     with jax.named_scope("two_exchange"):
         load = jnp.concatenate([wide(g2, "gy", 0, 8), jnp.pad(c3, ((0, 5), (0, 0)))])
-        load, c2lo, c2hi = lax.optimization_barrier((load, c2lo, c2hi))
+        far_lo, far_hi = lax.optimization_barrier((far_lo, far_hi, g2))[:2]
+        c2own = jnp.concatenate([far_lo, tlo[None], c2[None], thi[None], far_hi])
+        c2lo, c2hi = ring(c2own, "gy", 1), ring(c2own, "gy", -1)
+        load = after_all(load, c2own)
         g2e = everyone(load, "gx")
 
     with jax.named_scope("three_halo"):

time: 165 us -> 165 us (level)
    ppermute x32, waiting for transfers between devices: 38.5 us -> 41.4 us  [ring(): return lax.ppermute(value, axis, [(i, (i + step) % N) for i in range(N)])]
  transfers between devices with their start and end apart: 34 -> 34, of which waited for: 16 -> 14; matrix products, arithmetic and copies ran while one was open for 10% -> 11% of each run, Pallas kernels for 9% -> 9%
where the time goes in v3:
time: 165 us; the launch traced here: 164 us
  starting transfers between devices  62.3 us (38%)
  waiting for transfers between devices  47.9 us (29%)
  Pallas kernels  30.3 us (18%)
  local copies, waits for them, and re-layouts  13.8 us (8%)
  other arithmetic  8.78 us (5%)
    ppermute x32, starting transfers between devices, ring(): return lax.ppermute(value, axis, [(i, (i + step) % N) for i in range(N)])  48.3 us
    ppermute x32, waiting for transfers between devices, ring(): return lax.ppermute(value, axis, [(i, (i + step) % N) for i in range(N)])  41.4 us
    pallas_call x5, Pallas kernels, call(): pl.pallas_call(kernel, name=name, out_shape=shapes, in_specs=[pl.BlockSpe...  30.3 us
    all_to_all x2, starting transfers between devices, everyone(): return lax.all_to_all(copies, axis, 0, 0)  14 us
    all_to_all x2, waiting for transfers between devices, everyone(): return lax.all_to_all(copies, axis, 0, 0)  6.47 us
  transfers between devices with their start and end apart: 34, of which 14 were waited for; matrix products, arithmetic and copies ran while one was open for 11% of the time, Pallas kernels for 9%

profile of v3, /device:TPU:103, one launch (start us, length us, event | category | flops | bytes accessed | tf_op | source)
XLA Modules:
  0.0 163.8 jit_solution(5631606212840494658)
XLA Ops:
  4.8 3.0 %collective-permute-start.4 = (f32[1944,128]{1,0:T(8,128)}, f32[1944,128]{1,0:T(8,128)}, u32[]{:S(2)}, u32[]{:S(2)}) collective-permute-start(f32[1944,128]{1,0:T(8,128)} %maximum_maximum_fusion), channel_id=1, source_target_pairs={{0,16},{16,32},{32,48},{48,64},{64,80},{80,96},{96,112},{112,128},... | collective-permute-start | bytes 2985992 | tf_op jit(solution)/shard_map/two_three_halo/ppermute | solution.py:16
  7.8 5.0 %collective-permute-done.xlo = f32[2,7,32,256]{3,2,1,0:T(8,128)S(1)} collective-permute-done((f32[2,7,32,256]{3,2,1,0:T(8,128)S(1)}, f32[2,7,32,256]{3,2,1,0:T(8,128)S(1)}, u32[]{:S(2)}, u32[]{:S(2)}) %collective-permute-start) | collective-permute-done | bytes 458784 | tf_op jit(solution)/shard_map/fine_halo/ppermute | solution.py:16
  12.9 3.1 %collective-permute-done.1.xhi = f32[2,7,32,256]{3,2,1,0:T(8,128)S(1)} collective-permute-done((f32[2,7,32,256]{3,2,1,0:T(8,128)S(1)}, f32[2,7,32,256]{3,2,1,0:T(8,128)S(1)}, u32[]{:S(2)}, u32[]{:S(2)}) %collective-permute-start.1) | collective-permute-done | bytes 458784 | tf_op jit(solution)/shard_map/fine_halo/ppermute | solution.py:16
  16.1 6.1 %collective-permute-start.2 = (f32[2,22,8,256]{3,2,1,0:T(8,128)S(1)}, f32[2,22,8,256]{3,2,1,0:T(8,128)S(1)}, u32[]{:S(2)}, u32[]{:S(2)}) collective-permute-start(f32[2,22,8,256]{3,2,1,0:T(8,128)S(1)} %pad_maximum_fusion.11), channel_id=1, source_target_pairs={{0,1},{1,2},{2,3},{3,4},{4,5},{5,6},{6,7},{7,8},{8,9},{9,10},{10,1... | collective-permute-start | bytes 1081352 | tf_op jit(solution)/shard_map/fine_halo/ppermute | solution.py:16
  24.0 3.0 %collective-permute-start.6 = (f32[27,4,8,128]{3,2,1,0:T(8,128)}, f32[27,4,8,128]{3,2,1,0:T(8,128)}, u32[]{:S(2)}, u32[]{:S(2)}) collective-permute-start(f32[27,4,8,128]{3,2,1,0:T(8,128)} %get-tuple-element.80), channel_id=1, source_target_pairs={{0,1},{1,2},{2,3},{3,4},{4,5},{5,6},{6,7},{7,8},{8,9},{9,10},{10,1... | collective-permute-start | bytes 1327112 | tf_op jit(solution)/shard_map/fine_halo/ppermute | solution.py:16
  27.0 10.4 %collective-permute-done.3.yhi = f32[2,22,8,256]{3,2,1,0:T(8,128)S(1)} collective-permute-done((f32[2,22,8,256]{3,2,1,0:T(8,128)}, f32[2,22,8,256]{3,2,1,0:T(8,128)S(1)}, u32[]{:S(2)}, u32[]{:S(2)}) %collective-permute-start.3) | collective-permute-done | bytes 360480 | tf_op jit(solution)/shard_map/fine_halo/ppermute | solution.py:16
  37.4 6.6 %fine_down.1 = (f32[16,48,256]{2,1,0:T(8,128)S(1)}, f32[6,16,128]{2,1,0:T(8,128)S(1)}, f32[16,48,256]{2,1,0:T(8,128)S(1)}, f32[16,48,256]{2,1,0:T(8,128)}) custom-call(s32[2]{0:T(128)S(1)} %pad_add_fusion.pos, f32[8,32,256]{2,1,0:T(8,128)S(1)} %copy-done.4, f32[8,32,256]{2,1,0:T(8,128)S(1)} %copy-done.5, f32[2,7,32,256]{3,2,1,0:T(8,128)S(1)} %collective-permute-done.xlo, ...), custom_call_target="tpu_custom_call" | custom-call | tf_op jit(solution)/shard_map/fine_down/fine_down/pallas_call | solution.py:501
  50.1 2.9 %collective-permute-start.10 = (f32[1840,128]{1,0:T(8,128)S(1)}, f32[1840,128]{1,0:T(8,128)S(1)}, u32[]{:S(2)}, u32[]{:S(2)}) collective-permute-start(f32[1840,128]{1,0:T(8,128)S(1)} %pad_maximum_fusion.3), channel_id=1, source_target_pairs={{0,1},{1,2},{2,3},{3,4},{4,5},{5,6},{6,7},{7,8},{8,9},{9,10},{10,1... | collective-permute-start | bytes 2826248 | tf_op jit(solution)/shard_map/one_exchange/ppermute | solution.py:16
  55.2 2.8 %collective-permute-start.15 = (f32[2,216,128]{2,1,0:T(8,128)S(1)}, f32[2,216,128]{2,1,0:T(8,128)S(1)}, u32[]{:S(2)}, u32[]{:S(2)}) collective-permute-start(f32[2,216,128]{2,1,0:T(8,128)S(1)} %get-tuple-element.97), channel_id=1, source_target_pairs={{0,208},{16,224},{32,240},{48,0},{64,16},{80,32},{96,48},{112,64},... | collective-permute-start | bytes 663560 | tf_op jit(solution)/shard_map/two_halo/ppermute | solution.py:16
  58.0 1.7 %pad_maximum_fusion.cx = f32[27,12,16,128]{3,2,1,0:T(8,128)} fusion(f32[27,4,16,128]{3,2,1,0:T(8,128)S(1)} %bitcast.87, f32[27,4,16,128]{3,2,1,0:T(8,128)S(1)} %copy-done.13, f32[27,4,16,128]{3,2,1,0:T(8,128)S(1)} %bitcast.85), kind=kLoop, calls=%fused_computation | loop fusion | flops 1327104 | bytes 5308416 | tf_op jit(solution)/shard_map/one_down/concatenate | solution.py:595
  59.6 4.7 %collective-permute-done.11 = f32[1840,128]{1,0:T(8,128)S(1)} collective-permute-done((f32[1840,128]{1,0:T(8,128)S(1)}, f32[1840,128]{1,0:T(8,128)S(1)}, u32[]{:S(2)}, u32[]{:S(2)}) %collective-permute-start.11) | collective-permute-done | bytes 942112 | tf_op jit(solution)/shard_map/one_exchange/ppermute | solution.py:16
  67.3 5.9 %one_down.1 = (f32[8,128]{1,0:T(8,128)S(1)}, f32[4,16,128]{2,1,0:T(8,128)S(1)}) custom-call(s32[2]{0:T(128)S(1)} %pad_add_fusion.pos, f32[14,32,128]{2,1,0:T(8,128)S(1)} %pad_maximum_fusion.13.g.g1, f32[27,12,16,128]{3,2,1,0:T(8,128)} %pad_maximum_fusion.cx, f32[27,12,8,128]{3,2,1,0:T(8,128)S(1)} %pad_maximum_fusion.1.clo, ...), custom_call_target="tpu_custom_call" | custom-call | tf_op jit(solution)/shard_map/one_down/one_down/pallas_call | solution.py:501
  73.3 3.0 %collective-permute-start.12 = (f32[8,128]{1,0:T(8,128)S(1)}, f32[8,128]{1,0:T(8,128)S(1)}, u32[]{:S(2)}, u32[]{:S(2)}) collective-permute-start(f32[8,128]{1,0:T(8,128)S(1)} %get-tuple-element.54), channel_id=1, source_target_pairs={{0,1},{1,2},{2,3},{3,4},{4,5},{5,6},{6,7},{7,8},{8,9},{9,10},{10,1... | collective-permute-start | bytes 12296 | tf_op jit(solution)/shard_map/two_exchange/ppermute | solution.py:16
  76.5 2.9 %collective-permute-start.18 = (f32[7,216,128]{2,1,0:T(8,128)S(1)}, f32[7,216,128]{2,1,0:T(8,128)S(1)}, u32[]{:S(2)}, u32[]{:S(2)}) collective-permute-start(f32[7,216,128]{2,1,0:T(8,128)S(1)} %constant_dynamic-update-slice_fusion.c2own), channel_id=1, source_target_pairs={{0,1},{1,2},{2,3},{3,4},{4,5},{5,6},{6,7},{7,8},{8,9},{9,10},{10,1... | collective-permute-start | bytes 2322440 | tf_op jit(solution)/shard_map/two_exchange/ppermute | solution.py:16
  80.2 7.5 %all-to-all-start = ((f32[16,56,128]{2,1,0:T(8,128)}), f32[16,56,128]{2,1,0:T(8,128)S(1)}, u32[]{:S(2)}, u32[]{:S(2)}) async-start(f32[16,56,128]{2,1,0:T(8,128)} %broadcast_in_dim.4), calls=%async_computation | async-start | bytes 917504 | tf_op jit(solution)/shard_map/two_exchange/all_to_all | solution.py:21
  88.3 3.0 %collective-permute-start.20 = (f32[4,16,128]{2,1,0:T(8,128)S(1)}, f32[4,16,128]{2,1,0:T(8,128)S(1)}, u32[]{:S(2)}, u32[]{:S(2)}) collective-permute-start(f32[4,16,128]{2,1,0:T(8,128)S(1)} %get-tuple-element.63), channel_id=1, source_target_pairs={{0,16},{16,32},{32,48},{48,64},{64,80},{80,96},{96,112},{112,128},... | collective-permute-start | bytes 98312 | tf_op jit(solution)/shard_map/one_values/ppermute | solution.py:16
  91.3 3.8 %all-to-all-done.g_all.g2_all = f32[16,56,128]{2,1,0:T(8,128)S(1)} async-done(((f32[16,56,128]{2,1,0:T(8,128)}), f32[16,56,128]{2,1,0:T(8,128)S(1)}, u32[]{:S(2)}, u32[]{:S(2)}) %all-to-all-start) | async-done | bytes 458784 | tf_op jit(solution)/shard_map/two_exchange/all_to_all | solution.py:21
  96.0 2.9 %collective-permute-start.16 = (f32[432,128]{1,0:T(8,128)S(1)}, f32[432,128]{1,0:T(8,128)S(1)}, u32[]{:S(2)}, u32[]{:S(2)}) collective-permute-start(f32[432,128]{1,0:T(8,128)S(1)} %bitcast.96), channel_id=1, source_target_pairs={{0,1},{1,2},{2,3},{3,4},{4,5},{5,6},{6,7},{7,8},{8,9},{9,10},{10,1... | collective-permute-start | bytes 663560 | tf_op jit(solution)/shard_map/three_halo/ppermute | solution.py:16
  98.9 1.8 %two_down.1 = (f32[8,128]{1,0:T(8,128)S(1)}, f32[8,128]{1,0:T(8,128)S(1)}) custom-call(s32[2]{0:T(128)S(1)} %pad_add_fusion.pos, f32[16,56,128]{2,1,0:T(8,128)S(1)} %all-to-all-done.g_all.g2_all, f32[7,216,128]{2,1,0:T(8,128)S(1)} %collective-permute-done.18.c2lo, f32[7,216,128]{2,1,0:T(8,128)S(1)} %constant_dynamic-update-slice_fusion.c2own, ...), custom_call_target="tpu_custom_call" | custom-call | tf_op jit(solution)/shard_map/two_down/two_down/pallas_call | solution.py:501
  100.8 2.9 %collective-permute-start.22 = (f32[112,128]{1,0:T(8,128)S(1)}, f32[112,128]{1,0:T(8,128)S(1)}, u32[]{:S(2)}, u32[]{:S(2)}) collective-permute-start(f32[112,128]{1,0:T(8,128)S(1)} %get-tuple-element.120), channel_id=1, source_target_pairs={{0,1},{1,2},{2,3},{3,4},{4,5},{5,6},{6,7},{7,8},{8,9},{9,10},{10,1... | collective-permute-start | bytes 172040 | tf_op jit(solution)/shard_map/three_exchange/ppermute | solution.py:16
  103.8 1.8 %collective-permute-done.23 = f32[112,128]{1,0:T(8,128)S(1)} collective-permute-done((f32[112,128]{1,0:T(8,128)S(1)}, f32[112,128]{1,0:T(8,128)S(1)}, u32[]{:S(2)}, u32[]{:S(2)}) %collective-permute-start.23) | collective-permute-done | bytes 57376 | tf_op jit(solution)/shard_map/three_exchange/ppermute | solution.py:16
  105.7 2.7 %collective-permute-start.24 = (f32[3,128]{1,0:T(4,128)S(1)}, f32[3,128]{1,0:T(4,128)S(1)}, u32[]{:S(2)}, u32[]{:S(2)}) collective-permute-start(f32[3,128]{1,0:T(4,128)S(1)} %pad_maximum_fusion.23), channel_id=1, source_target_pairs={{0,2},{1,3},{2,4},{3,5},{4,6},{5,7},{6,8},{7,9},{8,10},{9,11},{10,... | collective-permute-start | bytes 4616 | tf_op jit(solution)/shard_map/three_exchange/ppermute | solution.py:16
  110.4 6.5 %all-to-all-start.1 = ((f32[16,32,128]{2,1,0:T(8,128)}), f32[16,32,128]{2,1,0:T(8,128)}, u32[]{:S(2)}, u32[]{:S(2)}) async-start(f32[16,32,128]{2,1,0:T(8,128)} %broadcast_in_dim.5), calls=%async_computation.1 | async-start | bytes 524288 | tf_op jit(solution)/shard_map/three_exchange/all_to_all | solution.py:21
  117.4 2.5 %collective-permute-start.26 = (f32[864,128]{1,0:T(8,128)}, f32[864,128]{1,0:T(8,128)S(1)}, u32[]{:S(2)}, u32[]{:S(2)}) collective-permute-start(f32[864,128]{1,0:T(8,128)} %bitcast.39), channel_id=1, source_target_pairs={{0,2},{1,3},{2,4},{3,5},{4,6},{5,7},{6,8},{7,9},{8,10},{9,11},{10,... | collective-permute-start | bytes 1327112 | tf_op jit(solution)/shard_map/three_exchange/ppermute | solution.py:16
  119.9 2.7 %all-to-all-done.1 = f32[16,32,128]{2,1,0:T(8,128)} async-done(((f32[16,32,128]{2,1,0:T(8,128)}), f32[16,32,128]{2,1,0:T(8,128)}, u32[]{:S(2)}, u32[]{:S(2)}) %all-to-all-start.1) | async-done | bytes 262176 | tf_op jit(solution)/shard_map/three_exchange/all_to_all | solution.py:21
  124.4 3.6 %collective-permute-done.26 = f32[864,128]{1,0:T(8,128)S(1)} collective-permute-done((f32[864,128]{1,0:T(8,128)}, f32[864,128]{1,0:T(8,128)S(1)}, u32[]{:S(2)}, u32[]{:S(2)}) %collective-permute-start.26) | collective-permute-done | bytes 442400 | tf_op jit(solution)/shard_map/three_exchange/ppermute | solution.py:16
  128.0 2.8 %collective-permute-done.27 = f32[864,128]{1,0:T(8,128)S(1)} collective-permute-done((f32[864,128]{1,0:T(8,128)}, f32[864,128]{1,0:T(8,128)S(1)}, u32[]{:S(2)}, u32[]{:S(2)}) %collective-permute-start.27) | collective-permute-done | bytes 442400 | tf_op jit(solution)/shard_map/three_exchange/ppermute | solution.py:16
  132.6 10.9 %coarse_up.1 = f32[4,16,128]{2,1,0:T(8,128)S(1)} custom-call(s32[2]{0:T(128)S(1)} %pad_add_fusion.pos, f32[7,16,128]{2,1,0:T(8,128)S(1)} %copy.19.g3, f32[16,24,128]{2,1,0:T(8,128)S(1)} %slice.272.v2, f32[2,27,16,128]{3,2,1,0:T(8,128)S(1)} %bitcast.82, f32[3,27,16,128]{3,2,1,0:T(8,128)S(1)} %copy.20.c3own, f32[2,27,16,128]{3,2,1,0:T(8,128)S(1)} %bitcast.83, ...), custom_call_target="tpu_custom_call" | custom-call | tf_op jit(solution)/shard_map/coarse_up/coarse_up/pallas_call | solution.py:501
  146.2 3.3 %collective-permute-done.29 = f32[3,16,128]{2,1,0:T(8,128)S(1)} collective-permute-done((f32[3,16,128]{2,1,0:T(8,128)S(1)}, f32[3,16,128]{2,1,0:T(8,128)S(1)}, u32[]{:S(2)}, u32[]{:S(2)}) %collective-permute-start.29) | collective-permute-done | bytes 24608 | tf_op jit(solution)/shard_map/one_back/ppermute | solution.py:16
  149.5 4.4 %collective-permute-start.30 = (f32[10,8,128]{2,1,0:T(8,128)S(1)}, f32[10,8,128]{2,1,0:T(8,128)S(1)}, u32[]{:S(2)}, u32[]{:S(2)}) collective-permute-start(f32[10,8,128]{2,1,0:T(8,128)S(1)} %get-tuple-element.107), channel_id=1, source_target_pairs={{0,1},{1,2},{2,3},{3,4},{4,5},{5,6},{6,7},{7,8},{8,9},{9,10},{10,1... | collective-permute-start | bytes 122888 | tf_op jit(solution)/shard_map/one_back/ppermute | solution.py:16
  155.1 3.5 %collective-permute-done.31 = f32[10,8,128]{2,1,0:T(8,128)S(1)} collective-permute-done((f32[10,8,128]{2,1,0:T(8,128)S(1)}, f32[10,8,128]{2,1,0:T(8,128)S(1)}, u32[]{:S(2)}, u32[]{:S(2)}) %collective-permute-start.31) | collective-permute-done | bytes 40992 | tf_op jit(solution)/shard_map/one_back/ppermute | solution.py:16
  158.7 5.1 %fine_up.1 = f32[8,32,256]{2,1,0:T(8,128)} custom-call(s32[2]{0:T(128)S(1)} %pad_add_fusion.pos, f32[16,48,256]{2,1,0:T(8,128)S(1)} %copy-done.9, f32[16,48,256]{2,1,0:T(8,128)S(1)} %copy-done.10, f32[16,48,256]{2,1,0:T(8,128)S(1)} %copy-done.7, f32[10,32,128]{2,1,0:T(8,128)S(1)} %pad_maximum_fusion.15.c1), custom_call_target="tpu_custom_call" | custom-call | tf_op jit(solution)/shard_map/fine_up/fine_up/pallas_call | solution.py:501
  (164 shorter events, 30.2 us)
Async XLA Ops:
  1.4 11.5 %collective-permute-start = (f32[2,7,32,256]{3,2,1,0:T(8,128)S(1)}, f32[2,7,32,256]{3,2,1,0:T(8,128)S(1)}, u32[]{:S(2)}, u32[]{:S(2)}) collective-permute-start(f32[2,7,32,256]{3,2,1,0:T(8,128)S(1)} %pad_maximum_fusion.7), channel_id=1, source_target_pairs={{0,16},{16,32},{32,48},{48,64},{64,80},{80,96},{96,112},{112,128},... | collective-permute-start | bytes 1376264 | tf_op jit(solution)/shard_map/fine_halo/ppermute | solution.py:16
  2.8 13.3 %collective-permute-start.1 = (f32[2,7,32,256]{3,2,1,0:T(8,128)S(1)}, f32[2,7,32,256]{3,2,1,0:T(8,128)S(1)}, u32[]{:S(2)}, u32[]{:S(2)}) collective-permute-start(f32[2,7,32,256]{3,2,1,0:T(8,128)S(1)} %pad_maximum_fusion.8), channel_id=1, source_target_pairs={{0,240},{16,0},{32,16},{48,32},{64,48},{80,64},{96,80},{112,96},{1... | collective-permute-start | bytes 1376264 | tf_op jit(solution)/shard_map/fine_halo/ppermute | solution.py:16
  4.2 39.7 %collective-permute-start.5 = (f32[1944,128]{1,0:T(8,128)}, f32[1944,128]{1,0:T(8,128)}, u32[]{:S(2)}, u32[]{:S(2)}) collective-permute-start(f32[1944,128]{1,0:T(8,128)} %maximum_maximum_fusion), channel_id=1, source_target_pairs={{0,240},{16,0},{32,16},{48,32},{64,48},{80,64},{96,80},{112,96},{1... | collective-permute-start | bytes 2985992 | tf_op jit(solution)/shard_map/two_three_halo/ppermute | solution.py:16
  4.8 39.2 %collective-permute-start.4 = (f32[1944,128]{1,0:T(8,128)}, f32[1944,128]{1,0:T(8,128)}, u32[]{:S(2)}, u32[]{:S(2)}) collective-permute-start(f32[1944,128]{1,0:T(8,128)} %maximum_maximum_fusion), channel_id=1, source_target_pairs={{0,16},{16,32},{32,48},{48,64},{64,80},{80,96},{96,112},{112,128},... | collective-permute-start | bytes 2985992 | tf_op jit(solution)/shard_map/two_three_halo/ppermute | solution.py:16
  16.1 10.8 %collective-permute-start.2 = (f32[2,22,8,256]{3,2,1,0:T(8,128)S(1)}, f32[2,22,8,256]{3,2,1,0:T(8,128)S(1)}, u32[]{:S(2)}, u32[]{:S(2)}) collective-permute-start(f32[2,22,8,256]{3,2,1,0:T(8,128)S(1)} %pad_maximum_fusion.11), channel_id=1, source_target_pairs={{0,1},{1,2},{2,3},{3,4},{4,5},{5,6},{6,7},{7,8},{8,9},{9,10},{10,1... | collective-permute-start | bytes 1081352 | tf_op jit(solution)/shard_map/fine_halo/ppermute | solution.py:16
  24.0 20.0 %collective-permute-start.7 = (f32[27,4,8,128]{3,2,1,0:T(8,128)}, f32[27,4,8,128]{3,2,1,0:T(8,128)}, u32[]{:S(2)}, u32[]{:S(2)}) collective-permute-start(f32[27,4,8,128]{3,2,1,0:T(8,128)} %get-tuple-element.79), channel_id=1, source_target_pairs={{0,15},{1,0},{2,1},{3,2},{4,3},{5,4},{6,5},{7,6},{8,7},{9,8},{10,9... | collective-permute-start | bytes 1327112 | tf_op jit(solution)/shard_map/fine_halo/ppermute | solution.py:16
  24.0 20.0 %collective-permute-start.6 = (f32[27,4,8,128]{3,2,1,0:T(8,128)}, f32[27,4,8,128]{3,2,1,0:T(8,128)}, u32[]{:S(2)}, u32[]{:S(2)}) collective-permute-start(f32[27,4,8,128]{3,2,1,0:T(8,128)} %get-tuple-element.80), channel_id=1, source_target_pairs={{0,1},{1,2},{2,3},{3,4},{4,5},{5,6},{6,7},{7,8},{8,9},{9,10},{10,1... | collective-permute-start | bytes 1327112 | tf_op jit(solution)/shard_map/fine_halo/ppermute | solution.py:16
  26.9 10.5 %collective-permute-start.3 = (f32[2,22,8,256]{3,2,1,0:T(8,128)}, f32[2,22,8,256]{3,2,1,0:T(8,128)S(1)}, u32[]{:S(2)}, u32[]{:S(2)}) collective-permute-start(f32[2,22,8,256]{3,2,1,0:T(8,128)} %pad_maximum_fusion.12), channel_id=1, source_target_pairs={{0,15},{1,0},{2,1},{3,2},{4,3},{5,4},{6,5},{7,6},{8,7},{9,8},{10,9... | collective-permute-start | bytes 1081352 | tf_op jit(solution)/shard_map/fine_halo/ppermute | solution.py:16
  44.8 4.2 %collective-permute-start.8 = (f32[5,16,128]{2,1,0:T(8,128)S(1)}, f32[5,16,128]{2,1,0:T(8,128)S(1)}, u32[]{:S(2)}, u32[]{:S(2)}) collective-permute-start(f32[5,16,128]{2,1,0:T(8,128)S(1)} %get-tuple-element.117), channel_id=1, source_target_pairs={{0,16},{16,32},{32,48},{48,64},{64,80},{80,96},{96,112},{112,128},... | collective-permute-start | bytes 122888 | tf_op jit(solution)/shard_map/one_exchange/ppermute | solution.py:16
  44.9 5.0 %collective-permute-start.9 = (f32[5,16,128]{2,1,0:T(8,128)S(1)}, f32[5,16,128]{2,1,0:T(8,128)S(1)}, u32[]{:S(2)}, u32[]{:S(2)}) collective-permute-start(f32[5,16,128]{2,1,0:T(8,128)S(1)} %get-tuple-element.118), channel_id=1, source_target_pairs={{0,240},{16,0},{32,16},{48,32},{64,48},{80,64},{96,80},{112,96},{1... | collective-permute-start | bytes 122888 | tf_op jit(solution)/shard_map/one_exchange/ppermute | solution.py:16
  50.0 14.3 %collective-permute-start.11 = (f32[1840,128]{1,0:T(8,128)S(1)}, f32[1840,128]{1,0:T(8,128)S(1)}, u32[]{:S(2)}, u32[]{:S(2)}) collective-permute-start(f32[1840,128]{1,0:T(8,128)S(1)} %pad_maximum_fusion.4), channel_id=1, source_target_pairs={{0,15},{1,0},{2,1},{3,2},{4,3},{5,4},{6,5},{7,6},{8,7},{9,8},{10,9... | collective-permute-start | bytes 2826248 | tf_op jit(solution)/shard_map/one_exchange/ppermute | solution.py:16
  50.1 14.3 %collective-permute-start.10 = (f32[1840,128]{1,0:T(8,128)S(1)}, f32[1840,128]{1,0:T(8,128)S(1)}, u32[]{:S(2)}, u32[]{:S(2)}) collective-permute-start(f32[1840,128]{1,0:T(8,128)S(1)} %pad_maximum_fusion.3), channel_id=1, source_target_pairs={{0,1},{1,2},{2,3},{3,4},{4,5},{5,6},{6,7},{7,8},{8,9},{9,10},{10,1... | collective-permute-start | bytes 2826248 | tf_op jit(solution)/shard_map/one_exchange/ppermute | solution.py:16
  55.2 21.1 %collective-permute-start.15 = (f32[2,216,128]{2,1,0:T(8,128)S(1)}, f32[2,216,128]{2,1,0:T(8,128)S(1)}, u32[]{:S(2)}, u32[]{:S(2)}) collective-permute-start(f32[2,216,128]{2,1,0:T(8,128)S(1)} %get-tuple-element.97), channel_id=1, source_target_pairs={{0,208},{16,224},{32,240},{48,0},{64,16},{80,32},{96,48},{112,64},... | collective-permute-start | bytes 663560 | tf_op jit(solution)/shard_map/two_halo/ppermute | solution.py:16
  58.0 18.3 %collective-permute-start.14 = (f32[2,216,128]{2,1,0:T(8,128)S(1)}, f32[2,216,128]{2,1,0:T(8,128)S(1)}, u32[]{:S(2)}, u32[]{:S(2)}) collective-permute-start(f32[2,216,128]{2,1,0:T(8,128)S(1)} %get-tuple-element.98), channel_id=1, source_target_pairs={{0,48},{16,64},{32,80},{48,96},{64,112},{80,128},{96,144},{112,160... | collective-permute-start | bytes 663560 | tf_op jit(solution)/shard_map/two_halo/ppermute | solution.py:16
  73.2 6.2 %collective-permute-start.13 = (f32[8,128]{1,0:T(8,128)S(1)}, f32[8,128]{1,0:T(8,128)S(1)}, u32[]{:S(2)}, u32[]{:S(2)}) collective-permute-start(f32[8,128]{1,0:T(8,128)S(1)} %get-tuple-element.54), channel_id=1, source_target_pairs={{0,15},{1,0},{2,1},{3,2},{4,3},{5,4},{6,5},{7,6},{8,7},{9,8},{10,9... | collective-permute-start | bytes 12296 | tf_op jit(solution)/shard_map/two_exchange/ppermute | solution.py:16
  73.3 6.2 %collective-permute-start.12 = (f32[8,128]{1,0:T(8,128)S(1)}, f32[8,128]{1,0:T(8,128)S(1)}, u32[]{:S(2)}, u32[]{:S(2)}) collective-permute-start(f32[8,128]{1,0:T(8,128)S(1)} %get-tuple-element.54), channel_id=1, source_target_pairs={{0,1},{1,2},{2,3},{3,4},{4,5},{5,6},{6,7},{7,8},{8,9},{9,10},{10,1... | collective-permute-start | bytes 12296 | tf_op jit(solution)/shard_map/two_exchange/ppermute | solution.py:16
  76.4 19.5 %collective-permute-start.19 = (f32[7,216,128]{2,1,0:T(8,128)S(1)}, f32[7,216,128]{2,1,0:T(8,128)S(1)}, u32[]{:S(2)}, u32[]{:S(2)}) collective-permute-start(f32[7,216,128]{2,1,0:T(8,128)S(1)} %constant_dynamic-update-slice_fusion.c2own), channel_id=1, source_target_pairs={{0,15},{1,0},{2,1},{3,2},{4,3},{5,4},{6,5},{7,6},{8,7},{9,8},{10,9... | collective-permute-start | bytes 2322440 | tf_op jit(solution)/shard_map/two_exchange/ppermute | solution.py:16
  76.5 22.4 %collective-permute-start.18 = (f32[7,216,128]{2,1,0:T(8,128)S(1)}, f32[7,216,128]{2,1,0:T(8,128)S(1)}, u32[]{:S(2)}, u32[]{:S(2)}) collective-permute-start(f32[7,216,128]{2,1,0:T(8,128)S(1)} %constant_dynamic-update-slice_fusion.c2own), channel_id=1, source_target_pairs={{0,1},{1,2},{2,3},{3,4},{4,5},{5,6},{6,7},{7,8},{8,9},{9,10},{10,1... | collective-permute-start | bytes 2322440 | tf_op jit(solution)/shard_map/two_exchange/ppermute | solution.py:16
  80.2 14.8 %all-to-all-start = ((f32[16,56,128]{2,1,0:T(8,128)}), f32[16,56,128]{2,1,0:T(8,128)S(1)}, u32[]{:S(2)}, u32[]{:S(2)}) async-start(f32[16,56,128]{2,1,0:T(8,128)} %broadcast_in_dim.4), calls=%async_computation | async-start | bytes 917504 | tf_op jit(solution)/shard_map/two_exchange/all_to_all | solution.py:21
  87.7 13.0 %collective-permute-start.21 = (f32[4,16,128]{2,1,0:T(8,128)S(1)}, f32[4,16,128]{2,1,0:T(8,128)S(1)}, u32[]{:S(2)}, u32[]{:S(2)}) collective-permute-start(f32[4,16,128]{2,1,0:T(8,128)S(1)} %get-tuple-element.63), channel_id=1, source_target_pairs={{0,240},{16,0},{32,16},{48,32},{64,48},{80,64},{96,80},{112,96},{1... | collective-permute-start | bytes 98312 | tf_op jit(solution)/shard_map/one_values/ppermute | solution.py:16
  88.3 12.4 %collective-permute-start.20 = (f32[4,16,128]{2,1,0:T(8,128)S(1)}, f32[4,16,128]{2,1,0:T(8,128)S(1)}, u32[]{:S(2)}, u32[]{:S(2)}) collective-permute-start(f32[4,16,128]{2,1,0:T(8,128)S(1)} %get-tuple-element.63), channel_id=1, source_target_pairs={{0,16},{16,32},{32,48},{48,64},{64,80},{80,96},{96,112},{112,128},... | collective-permute-start | bytes 98312 | tf_op jit(solution)/shard_map/one_values/ppermute | solution.py:16
  95.9 7.9 %collective-permute-start.17 = (f32[432,128]{1,0:T(8,128)S(1)}, f32[432,128]{1,0:T(8,128)S(1)}, u32[]{:S(2)}, u32[]{:S(2)}) collective-permute-start(f32[432,128]{1,0:T(8,128)S(1)} %bitcast.95), channel_id=1, source_target_pairs={{0,15},{1,0},{2,1},{3,2},{4,3},{5,4},{6,5},{7,6},{8,7},{9,8},{10,9... | collective-permute-start | bytes 663560 | tf_op jit(solution)/shard_map/three_halo/ppermute | solution.py:16
  96.0 7.8 %collective-permute-start.16 = (f32[432,128]{1,0:T(8,128)S(1)}, f32[432,128]{1,0:T(8,128)S(1)}, u32[]{:S(2)}, u32[]{:S(2)}) collective-permute-start(f32[432,128]{1,0:T(8,128)S(1)} %bitcast.96), channel_id=1, source_target_pairs={{0,1},{1,2},{2,3},{3,4},{4,5},{5,6},{6,7},{7,8},{8,9},{9,10},{10,1... | collective-permute-start | bytes 663560 | tf_op jit(solution)/shard_map/three_halo/ppermute | solution.py:16
  100.8 4.8 %collective-permute-start.23 = (f32[112,128]{1,0:T(8,128)S(1)}, f32[112,128]{1,0:T(8,128)S(1)}, u32[]{:S(2)}, u32[]{:S(2)}) collective-permute-start(f32[112,128]{1,0:T(8,128)S(1)} %get-tuple-element.119), channel_id=1, source_target_pairs={{0,15},{1,0},{2,1},{3,2},{4,3},{5,4},{6,5},{7,6},{8,7},{9,8},{10,9... | collective-permute-start | bytes 172040 | tf_op jit(solution)/shard_map/three_exchange/ppermute | solution.py:16
  100.8 4.8 %collective-permute-start.22 = (f32[112,128]{1,0:T(8,128)S(1)}, f32[112,128]{1,0:T(8,128)S(1)}, u32[]{:S(2)}, u32[]{:S(2)}) collective-permute-start(f32[112,128]{1,0:T(8,128)S(1)} %get-tuple-element.120), channel_id=1, source_target_pairs={{0,1},{1,2},{2,3},{3,4},{4,5},{5,6},{6,7},{7,8},{8,9},{9,10},{10,1... | collective-permute-start | bytes 172040 | tf_op jit(solution)/shard_map/three_exchange/ppermute | solution.py:16
  105.7 3.9 %collective-permute-start.25 = (f32[3,128]{1,0:T(4,128)S(1)}, f32[3,128]{1,0:T(4,128)S(1)}, u32[]{:S(2)}, u32[]{:S(2)}) collective-permute-start(f32[3,128]{1,0:T(4,128)S(1)} %pad_maximum_fusion.23), channel_id=1, source_target_pairs={{0,14},{1,15},{2,0},{3,1},{4,2},{5,3},{6,4},{7,5},{8,6},{9,7},{10,... | collective-permute-start | bytes 4616 | tf_op jit(solution)/shard_map/three_exchange/ppermute | solution.py:16
  110.4 12.2 %all-to-all-start.1 = ((f32[16,32,128]{2,1,0:T(8,128)}), f32[16,32,128]{2,1,0:T(8,128)}, u32[]{:S(2)}, u32[]{:S(2)}) async-start(f32[16,32,128]{2,1,0:T(8,128)} %broadcast_in_dim.5), calls=%async_computation.1 | async-start | bytes 524288 | tf_op jit(solution)/shard_map/three_exchange/all_to_all | solution.py:21
  117.4 10.6 %collective-permute-start.26 = (f32[864,128]{1,0:T(8,128)}, f32[864,128]{1,0:T(8,128)S(1)}, u32[]{:S(2)}, u32[]{:S(2)}) collective-permute-start(f32[864,128]{1,0:T(8,128)} %bitcast.39), channel_id=1, source_target_pairs={{0,2},{1,3},{2,4},{3,5},{4,6},{5,7},{6,8},{7,9},{8,10},{9,11},{10,... | collective-permute-start | bytes 1327112 | tf_op jit(solution)/shard_map/three_exchange/ppermute | solution.py:16
  119.9 10.9 %collective-permute-start.27 = (f32[864,128]{1,0:T(8,128)}, f32[864,128]{1,0:T(8,128)S(1)}, u32[]{:S(2)}, u32[]{:S(2)}) collective-permute-start(f32[864,128]{1,0:T(8,128)} %bitcast.41), channel_id=1, source_target_pairs={{0,14},{1,15},{2,0},{3,1},{4,2},{5,3},{6,4},{7,5},{8,6},{9,7},{10,... | collective-permute-start | bytes 1327112 | tf_op jit(solution)/shard_map/three_exchange/ppermute | solution.py:16
  144.7 4.8 %collective-permute-start.29 = (f32[3,16,128]{2,1,0:T(8,128)S(1)}, f32[3,16,128]{2,1,0:T(8,128)S(1)}, u32[]{:S(2)}, u32[]{:S(2)}) collective-permute-start(f32[3,16,128]{2,1,0:T(8,128)S(1)} %get-tuple-element.116), channel_id=1, source_target_pairs={{0,240},{16,0},{32,16},{48,32},{64,48},{80,64},{96,80},{112,96},{1... | collective-permute-start | bytes 73736 | tf_op jit(solution)/shard_map/one_back/ppermute | solution.py:16
  149.5 5.5 %collective-permute-start.30 = (f32[10,8,128]{2,1,0:T(8,128)S(1)}, f32[10,8,128]{2,1,0:T(8,128)S(1)}, u32[]{:S(2)}, u32[]{:S(2)}) collective-permute-start(f32[10,8,128]{2,1,0:T(8,128)S(1)} %get-tuple-element.107), channel_id=1, source_target_pairs={{0,1},{1,2},{2,3},{3,4},{4,5},{5,6},{6,7},{7,8},{8,9},{9,10},{10,1... | collective-permute-start | bytes 122888 | tf_op jit(solution)/shard_map/one_back/ppermute | solution.py:16
  154.0 4.6 %collective-permute-start.31 = (f32[10,8,128]{2,1,0:T(8,128)S(1)}, f32[10,8,128]{2,1,0:T(8,128)S(1)}, u32[]{:S(2)}, u32[]{:S(2)}) collective-permute-start(f32[10,8,128]{2,1,0:T(8,128)S(1)} %get-tuple-element.108), channel_id=1, source_target_pairs={{0,15},{1,0},{2,1},{3,2},{4,3},{5,4},{6,5},{7,6},{8,7},{9,8},{10,9... | collective-permute-start | bytes 122888 | tf_op jit(solution)/shard_map/one_back/ppermute | solution.py:16
  (25 other events, 285.0 us)
